TPU v7x, 512 devices: a whole 4x4x16 slice. The times are simulated.
512 devices in a mesh: row: 16 (over y, z_hi), col: 32 (over x, z_lo, core).
Axes of the slice: x: 4, y: 4, z: 16 (z_hi: 4, z_lo: 4; z = z_hi * 4 + z_lo), core: 2. Of those that a mesh axis runs over, the one named last changes fastest.
Arguments:
- nodes: bfloat16 [1024, 768], P('col'), may hold values from -6 to 6
- node_gain: float32 [768], replicated, may hold values from 0.25 to 1.75
- w_qkv: bfloat16 [3, 768, 768], P(None, None, 'row'), may hold values from -0.21875 to 0.21875
- w_out: bfloat16 [768, 768], P(None, 'col'), may hold values from -0.4375 to 0.4375
- pair: bfloat16 [1024, 1024, 128], P('row', 'col'), may hold values from -16 to 16
- pair_gain: float32 [128], replicated, may hold values from 0.25 to 1.75
- w_bias: bfloat16 [128, 16], replicated, may hold values from -10 to 10, as said below
- w_gate: bfloat16 [128, 16], replicated, may hold values from -0.5 to 0.5
- b_gate: float32 [16], replicated, may hold values from -1 to 3
- w_in: bfloat16 [256, 512], replicated, may hold values from -0.375 to 0.375
- b_in: float32 [512], replicated, may hold values from -3 to 3
- w_mlp_out: bfloat16 [512, 128], replicated, may hold values from -0.25 to 0.25
- b_out: float32 [128], replicated, may hold values from -3 to 3
Outputs:
- node_update: bfloat16 [1024, 768], P('row', 'col')
- pair_out: bfloat16 [1024, 1024, 128], P('row', 'col')
Inputs may be any that keep to these rules, and one draw needn't show every extreme that they name: `w_bias`: entries are of order 2.2 / sqrt(128).
All inputs are finite; a program needn't handle non-finite values.
Results may differ from a plain program's by a relative error of at most 0.011.
Values may be sent and summed in bfloat16 or wider, within the bound.
No kernel may reach another device: no remote copies, remote signals or barrier semaphores. Data moves between devices by JAX's collectives and lax.ppermute only.
A program may use at most 64 MiB of HBM per device.

v0:
```python
import math

import jax
import jax.numpy as jnp
from jax import lax
from jax.sharding import PartitionSpec as P


def merged(part, axis, combine):
    gathered = jax.tree.map(lambda a: lax.all_gather(a, axis), part)

    def take(source):
        return jax.tree.map(lambda a: lax.dynamic_index_in_dim(a, source, 0, False), gathered)

    return lax.fori_loop(
        1, lax.axis_size(axis), lambda source, state: combine(state, take(source)), take(0)
    )


def layer_norm(values_in, scale_gain):
    centred = values_in.astype(jnp.float32)
    centred = centred - jnp.mean(centred, axis=-1, keepdims=True)
    variance = jnp.mean(centred * centred, axis=-1, keepdims=True)
    return centred * lax.rsqrt(variance + 1e-05) * scale_gain


def combine(earlier, later):
    peak = jnp.maximum(earlier[0], later[0])
    factor_one = jnp.exp(earlier[0] - peak)
    factor_two = jnp.exp(later[0] - peak)
    return (
        peak,
        earlier[1] * factor_one + later[1] * factor_two,
        earlier[2] * factor_one[:, :, None] + later[2] * factor_two[:, :, None],
    )


def body(
    nodes,
    node_gain,
    w_qkv,
    w_out,
    pair,
    pair_gain,
    w_bias,
    w_gate,
    b_gate,
    w_in,
    b_in,
    w_mlp_out,
    b_out,
):
    key_rows = nodes.shape[0]
    node_width = nodes.shape[1]
    row_rows = pair.shape[0]
    key_cols = pair.shape[1]
    pair_width = pair.shape[2]
    head_count = w_bias.shape[1]
    head_size = node_width // head_count
    normed = layer_norm(nodes, node_gain).astype(jnp.bfloat16)
    local_proj = jnp.einsum(
        "nd,kde->kne", normed, w_qkv, preferred_element_type=jnp.float32
    ).astype(jnp.bfloat16)
    projected = lax.all_gather(local_proj, "row", axis=2, tiled=True)
    own_queries = projected[0]
    everyone = lax.all_gather(own_queries, "col", axis=0, tiled=True)
    queries = lax.dynamic_slice_in_dim(everyone, lax.axis_index("row") * row_rows, row_rows, 0)
    zed = layer_norm(pair, pair_gain).astype(jnp.bfloat16)
    halves = pair.reshape(2, key_cols, key_cols, pair_width)
    moved = lax.all_to_all(
        lax.all_to_all(halves, "row", split_axis=1, concat_axis=0, tiled=True),
        "col",
        split_axis=0,
        concat_axis=0,
        tiled=True,
    )
    settled = lax.all_to_all(moved, "row", split_axis=0, concat_axis=1, tiled=True)
    reverse_tile = jnp.transpose(settled, (0, 2, 1, 3)).reshape(row_rows, key_cols, pair_width)
    zed_reverse = layer_norm(reverse_tile, pair_gain).astype(jnp.bfloat16)
    query_heads = queries.reshape(row_rows, head_count, head_size)
    key_heads = projected[1].reshape(key_rows, head_count, head_size)
    value_heads = projected[2].reshape(key_rows, head_count, head_size)
    scores = jnp.einsum(
        "ihe,jhe->hij", query_heads, key_heads, preferred_element_type=jnp.float32
    ) / math.sqrt(head_size)
    pair_bias = jnp.einsum("ijc,ch->hij", pair, w_bias, preferred_element_type=jnp.float32)
    gate_prob = jax.nn.sigmoid(
        jnp.einsum("ijc,ch->hij", zed, w_gate, preferred_element_type=jnp.float32)
        + b_gate[:, None, None]
    )
    logits = scores + pair_bias
    top_score = jnp.max(logits, axis=2).T
    expo_score = jnp.exp(logits - top_score.T[:, :, None])
    denom_sum = jnp.sum(expo_score, axis=2).T
    weights = (expo_score * gate_prob).astype(jnp.bfloat16)
    weighted_sum = jnp.einsum(
        "hij,jhe->ihe", weights, value_heads, preferred_element_type=jnp.float32
    )
    top_score, denom_sum, weighted_sum = merged(
        (top_score, denom_sum, weighted_sum), "col", combine
    )
    attended = (
        (weighted_sum / denom_sum[:, :, None]).reshape(row_rows, node_width).astype(jnp.bfloat16)
    )
    node_update = jnp.dot(attended, w_out, preferred_element_type=jnp.float32).astype(jnp.bfloat16)
    block_rows = row_rows // 4
    pieces_out = []
    for piece_index in range(4):
        lower = piece_index * block_rows
        joined = jnp.concatenate(
            [zed[lower : lower + block_rows], zed_reverse[lower : lower + block_rows]], axis=-1
        )
        joined = joined.reshape(block_rows * key_cols, 2 * pair_width)
        hidden = jax.nn.gelu(
            jnp.dot(joined, w_in, preferred_element_type=jnp.float32) + b_in
        ).astype(jnp.bfloat16)
        update = jnp.dot(hidden, w_mlp_out, preferred_element_type=jnp.float32) + b_out
        updated = pair[lower : lower + block_rows].astype(jnp.float32) + update.reshape(
            block_rows, key_cols, pair_width
        )
        pieces_out.append(updated.astype(jnp.bfloat16))
    pair_out = jnp.concatenate(pieces_out, axis=0)
    return (node_update, pair_out)


def solution(mesh):
    return jax.shard_map(
        body,
        mesh=mesh,
        in_specs=(
            P("col", None),
            P(),
            P(None, None, "row"),
            P(None, "col"),
            P("row", "col", None),
            P(),
            P(),
            P(),
            P(),
            P(),
            P(),
            P(),
            P(),
        ),
        out_specs=(P("row", "col"), P("row", "col", None)),
        check_vma=False,
    )
```

profile of v0, /device:TPU:1, one launch (start us, length us, event | category | flops | bytes accessed | tf_op | source)
XLA Modules:
  0.0 389.3 jit_solution(14901745427853393001)
XLA Ops:
  7.2 2.0 copy.119
  9.2 18.5 %all-to-all-start = ((bf16[2,32,32,128]{3,2,0,1:T(8,128)(2,1)}), bf16[2,32,32,128]{3,2,0,1:T(8,128)(2,1)S(1)}, u32[]{:S(2)}, u32[]{:S(2)}) async-start(bf16[2,32,32,128]{3,2,0,1:T(8,128)(2,1)} %copy.119), calls=%async_computation | async-start | bytes 1048576 | tf_op jit(solution)/shard_map/all_to_all | solution.py:71
  29.6 25.3 %all-to-all-done = bf16[2,32,32,128]{3,2,0,1:T(8,128)(2,1)S(1)} async-done(((bf16[2,32,32,128]{3,2,0,1:T(8,128)(2,1)}), bf16[2,32,32,128]{3,2,0,1:T(8,128)(2,1)S(1)}, u32[]{:S(2)}, u32[]{:S(2)}) %all-to-all-start) | async-done | bytes 524320 | tf_op jit(solution)/shard_map/all_to_all | solution.py:71
  55.8 13.2 %all-to-all-start.1 = ((bf16[32,2,32,128]{3,2,1,0:T(8,128)(2,1)}), bf16[32,2,32,128]{3,2,1,0:T(8,128)(2,1)}, u32[]{:S(2)}, u32[]{:S(2)}) async-start(bf16[32,2,32,128]{3,2,1,0:T(8,128)(2,1)} %bitcast.21), calls=%async_computation.1 | async-start | bytes 1048576 | tf_op jit(solution)/shard_map/all_to_all | solution.py:70
  70.4 56.9 %all_gather.24 = bf16[3,32,768]{1,0,2:T(4,128)(2,1)S(1)} all-gather(bf16[3,32,48]{1,0,2:T(4,128)(2,1)S(1)} %copy.107), channel_id=1, replica_groups=mesh['row'=16,'col'=32] {'row'}, dimensions={2}, use_global_device_ids=true | all-gather | bytes 156672 | tf_op jit(solution)/shard_map/all_gather | solution.py:64
  129.1 10.8 %all-to-all-start.2 = ((bf16[32,2,32,128]{3,2,1,0:T(8,128)(2,1)}), bf16[32,2,32,128]{3,2,1,0:T(8,128)(2,1)S(1)}, u32[]{:S(2)}, u32[]{:S(2)}) async-start(bf16[32,2,32,128]{3,2,1,0:T(8,128)(2,1)} %all-to-all-done.1), calls=%async_computation.2 | async-start | bytes 1048576 | tf_op jit(solution)/shard_map/all_to_all | solution.py:77
  141.4 1.7 fusion.7
  143.1 1.6 fusion.45
  144.7 70.1 %all-gather.9.cloned.1.call-done = bf16[1,1024,768]{2,1,0:T(8,128)(2,1)} async-done(((bf16[1,32,768]{2,1,0:T(8,128)(2,1)}), bf16[1,1024,768]{2,1,0:T(8,128)(2,1)}) %all-gather.9.cloned.1.call-update) | async-done | bytes 1572880 | tf_op jit(solution)/shard_map/all_gather | solution.py:66
  222.0 43.5 %all-gather.4 = f32[32,64,16]{1,2,0:T(8,128)S(1)} all-gather(f32[1,64,16]{1,2,0:T(8,128)S(1)} %bitcast.120), channel_id=3, replica_groups=mesh['row'=16,'col'=32] {'col'}, dimensions={0}, use_global_device_ids=true | all-gather | bytes 135168 | tf_op jit(solution)/shard_map/all_gather | solution.py:10
  265.6 42.2 %all-gather.5 = f32[32,64,16]{1,2,0:T(8,128)S(1)} all-gather(f32[1,64,16]{1,2,0:T(8,128)S(1)} %bitcast.121), channel_id=4, replica_groups=mesh['row'=16,'col'=32] {'col'}, dimensions={0}, use_global_device_ids=true | all-gather | bytes 135168 | tf_op jit(solution)/shard_map/all_gather | solution.py:10
  308.1 1.6 convolution_add_fusion.7
  309.6 1.6 convolution_add_fusion.4
  311.2 1.6 convolution_add_fusion.5
  312.8 1.6 convolution_add_fusion.6
  315.4 13.4 %all-gather.11.cloned.1.call-done = f32[2048,16,48]{2,1,0:T(8,128)} async-done(((f32[64,16,48]{2,1,0:T(8,128)}), f32[2048,16,48]{2,1,0:T(8,128)}) %all-gather.11.cloned.1.call-update) | async-done | bytes 6291472 | tf_op jit(solution)/shard_map/all_gather | solution.py:10
  329.9 51.2 %while.19 = (s32[]{:T(128)}, f32[64,16]{0,1:T(8,128)S(1)}, f32[64,16]{0,1:T(8,128)S(1)}, f32[64,16,48]{2,1,0:T(8,128)S(1)}, f32[32,64,16]{1,2,0:T(8,128)S(1)}, /...) while((s32[]{:T(128)}, f32[64,16]{0,1:T(8,128)S(1)}, ...), condition=%wide.region_7.0_spmd, body=%wide.region_6.0_spmd.sunk | while | flops 153605 | bytes 647311 | solution.py:15
  330.1 1.4 fusion.130
  331.8 1.4 fusion.130
  333.4 1.4 fusion.130
  335.1 1.4 fusion.130
  340.0 1.4 fusion.130
  364.8 1.4 fusion.130
  371.4 1.4 fusion.130
  (185 shorter events, 58.4 us)
Async XLA Ops:
  7.2 300.9 %copy-start = (bf16[256,512]{1,0:T(8,128)(2,1)S(1)}, bf16[256,512]{1,0:T(8,128)(2,1)}, u32[]{:S(2)}) copy-start(bf16[256,512]{1,0:T(8,128)(2,1)} %param.24) | copy-start | bytes 786436
  7.2 211.0 %copy-start.1 = (bf16[64,32,128]{2,1,0:T(8,128)(2,1)S(1)}, bf16[64,32,128]{2,1,0:T(8,128)(2,1)}, u32[]{:S(2)}) copy-start(bf16[64,32,128]{2,1,0:T(8,128)(2,1)} %param.19) | copy-start | bytes 1572868
  7.2 211.0 %copy-start.4 = (f32[128]{0:T(128)S(1)}, f32[128]{0:T(128)}, u32[]{:S(2)}) copy-start(f32[128]{0:T(128)} %param.20) | copy-start | bytes 1540
  7.2 212.3 %copy-start.3 = (bf16[128,16]{0,1:T(8,128)(2,1)S(1)}, bf16[128,16]{0,1:T(8,128)(2,1)}, u32[]{:S(2)}) copy-start(bf16[128,16]{0,1:T(8,128)(2,1)} %param.22) | copy-start | bytes 12292
  7.2 213.4 %copy-start.6 = (f32[16]{0:T(128)S(1)}, f32[16]{0:T(128)}, u32[]{:S(2)}) copy-start(f32[16]{0:T(128)} %param.23) | copy-start | bytes 196
  9.2 298.8 %copy-start.5 = (f32[512]{0:T(512)S(1)}, f32[512]{0:T(512)}, u32[]{:S(2)}) copy-start(f32[512]{0:T(512)} %param.25) | copy-start | bytes 6148
  9.2 298.9 %copy-start.7 = (f32[128]{0:T(128)S(1)}, f32[128]{0:T(128)}, u32[]{:S(2)}) copy-start(f32[128]{0:T(128)} %param.27) | copy-start | bytes 1540
  9.2 45.7 %all-to-all-start = ((bf16[2,32,32,128]{3,2,0,1:T(8,128)(2,1)}), bf16[2,32,32,128]{3,2,0,1:T(8,128)(2,1)S(1)}, u32[]{:S(2)}, u32[]{:S(2)}) async-start(bf16[2,32,32,128]{3,2,0,1:T(8,128)(2,1)} %copy.119), calls=%async_computation | async-start | bytes 1048576 | tf_op jit(solution)/shard_map/all_to_all | solution.py:71
  55.8 73.3 %all-to-all-start.1 = ((bf16[32,2,32,128]{3,2,1,0:T(8,128)(2,1)}), bf16[32,2,32,128]{3,2,1,0:T(8,128)(2,1)}, u32[]{:S(2)}, u32[]{:S(2)}) async-start(bf16[32,2,32,128]{3,2,1,0:T(8,128)(2,1)} %bitcast.21), calls=%async_computation.1 | async-start | bytes 1048576 | tf_op jit(solution)/shard_map/all_to_all | solution.py:70
  69.0 145.7 %all-gather.9.cloned.1.call-start = ((), (), s32[]{:S(2)}) async-start(), calls=%async_computation.3 | async-start | bytes 1622016 | tf_op jit(solution)/shard_map/all_gather | solution.py:66
  129.1 87.0 %all-to-all-start.2 = ((bf16[32,2,32,128]{3,2,1,0:T(8,128)(2,1)}), bf16[32,2,32,128]{3,2,1,0:T(8,128)(2,1)S(1)}, u32[]{:S(2)}, u32[]{:S(2)}) async-start(bf16[32,2,32,128]{3,2,1,0:T(8,128)(2,1)} %all-to-all-done.1), calls=%async_computation.2 | async-start | bytes 1048576 | tf_op jit(solution)/shard_map/all_to_all | solution.py:77
  139.9 189.0 %all-gather.11.cloned.1.call-start = ((), (), s32[]{:S(2)}) async-start(), calls=%async_computation.4 | async-start | bytes 17301504 | tf_op jit(solution)/shard_map/all_gather | solution.py:10
  222.0 159.7 %copy-start.2 = (bf16[768,24]{0,1:T(8,128)(2,1)S(1)}, bf16[768,24]{0,1:T(8,128)(2,1)}, u32[]{:S(2)}) copy-start(bf16[768,24]{0,1:T(8,128)(2,1)} %param.18) | copy-start | bytes 110596
Sparse Core Ops, SparseCore 0:
  129.2 85.5 all-gather.8
  222.1 106.6 all-gather.10
where the time goes:
time: 392 us; the launch traced here: 389 us
  blocking collectives  143 us (36%)
  waiting for transfers between devices  109 us (28%)
  other arithmetic  54.1 us (14%)
  starting transfers between devices  42.6 us (11%)
  local copies, waits for them, and re-layouts  14.6 us (4%)
  between operations  14.4 us (4%)
  matrix products  11.2 us (3%)
    all_gather x2, blocking collectives, merged(): gathered = jax.tree.map(lambda a: lax.all_gather(a, axis), part)  85.7 us
    all_gather x1, waiting for transfers between devices, body(): everyone = lax.all_gather(own_queries, 'col', axis=0, tiled=True)  70.1 us
    all_gather x1, blocking collectives, body(): projected = lax.all_gather(local_proj, 'row', axis=2, tiled=True)  56.9 us
    add x31, other arithmetic, combine(): earlier[2] * factor_one[:, :, None] + later[2] * factor_two[:, :, None]  44.5 us
    all_to_all x1, waiting for transfers between devices, body(): lax.all_to_all(halves, 'row', split_axis=1, concat_axis=0, tiled=True)  25.3 us
    all_to_all x1, starting transfers between devices, body(): lax.all_to_all(halves, 'row', split_axis=1, concat_axis=0, tiled=True)  18.5 us
    all_gather x1, waiting for transfers between devices, merged(): gathered = jax.tree.map(lambda a: lax.all_gather(a, axis), part)  13.4 us
    all_to_all x1, starting transfers between devices, body(): lax.all_to_all(lax.all_to_all(halves, 'row', split_axis=1, concat_axis=0,...  13.2 us
  transfers between devices with their start and end apart: 5, of which 3 were waited for; matrix products, arithmetic and copies ran while one was open for 5% of the time, Pallas kernels for 0%

commit v1 on v0

v1 whole, which is shorter than its diff:
```python
import math

import jax
import jax.numpy as jnp
from jax import lax
from jax.sharding import PartitionSpec as P

F32 = jnp.float32
BF16 = jnp.bfloat16


def rounded(values):
    return lax.reduce_precision(values, 8, 7)


def layer_norm(values_in, scale_gain):
    centred = values_in.astype(F32)
    centred = centred - jnp.mean(centred, axis=-1, keepdims=True)
    variance = jnp.mean(centred * centred, axis=-1, keepdims=True)
    return centred * lax.rsqrt(variance + 1e-05) * scale_gain


def body(
    nodes,
    node_gain,
    w_qkv,
    w_out,
    pair,
    pair_gain,
    w_bias,
    w_gate,
    b_gate,
    w_in,
    b_in,
    w_mlp_out,
    b_out,
):
    rows_n = lax.axis_size("row")
    cols_n = lax.axis_size("col")
    key_rows, node_width = nodes.shape
    row_rows, key_cols, pair_width = pair.shape
    heads = w_bias.shape[1]
    head_size = node_width // heads
    half = key_rows // 2
    col = lax.axis_index("col")

    normed = layer_norm(nodes, node_gain).astype(BF16)
    proj = jnp.einsum("nd,kde->kne", normed, w_qkv, preferred_element_type=F32).astype(BF16)
    packed = jnp.concatenate([proj[:, :half], proj[:, half:]], axis=-1)
    spread = jnp.broadcast_to(packed[0][None], (cols_n,) + packed.shape[1:])
    all_q = lax.all_to_all(spread, "col", 0, 0, tiled=True)

    zed = layer_norm(pair, pair_gain).astype(BF16)
    zed_t = jnp.transpose(zed, (1, 0, 2))
    odd = col % 2
    first = lax.dynamic_slice_in_dim(zed_t, odd * key_cols, key_cols, 1)
    second = lax.dynamic_slice_in_dim(zed_t, (1 - odd) * key_cols, key_cols, 1)
    same = [
        (r * cols_n + c, (c // 2) * cols_n + 2 * r + c % 2)
        for r in range(rows_n)
        for c in range(cols_n)
    ]
    swap = [
        (r * cols_n + c, (c // 2) * cols_n + 2 * r + 1 - c % 2)
        for r in range(rows_n)
        for c in range(cols_n)
    ]
    back_one = lax.ppermute(first, ("row", "col"), same)
    back_two = lax.ppermute(second, ("row", "col"), swap)

    own_kv = jnp.concatenate([packed[1], packed[2]], axis=0)
    sent = jnp.concatenate(
        [
            all_q.reshape(rows_n, 2 * half, 2 * head_size),
            jnp.broadcast_to(own_kv[None], (rows_n,) + own_kv.shape),
        ],
        axis=1,
    )
    got = lax.all_to_all(sent, "row", 0, 0, tiled=True)

    def unpack(piece, blocks):
        piece = piece.reshape(heads, blocks, half, 2, head_size)
        return jnp.transpose(piece, (0, 1, 3, 2, 4)).reshape(heads, blocks * key_rows, head_size)

    query = unpack(got[:, : 2 * half], 2)
    key = unpack(got[:, 2 * half : 3 * half], 1)
    value = unpack(got[:, 3 * half :], 1)

    scores = jnp.einsum("hie,hje->hij", query, key, preferred_element_type=F32) / math.sqrt(head_size)
    pair_bias = jnp.einsum("ijc,ch->hij", pair, w_bias, preferred_element_type=F32)
    gate_prob = jax.nn.sigmoid(
        jnp.einsum("ijc,ch->hij", zed, w_gate, preferred_element_type=F32) + b_gate[:, None, None]
    )
    logits = scores + pair_bias
    peak = jnp.max(logits, axis=2)
    peak_hi = rounded(peak)
    peak_lo = rounded(peak - peak_hi)
    expo = jnp.exp(logits - (peak_hi + peak_lo)[:, :, None])
    denom = jnp.sum(expo, axis=2)
    weights = (expo * gate_prob).astype(BF16)
    part = jnp.einsum("hij,hje->ihe", weights, value, preferred_element_type=F32)
    denom_hi = rounded(denom)
    denom_lo = rounded(denom - denom_hi)
    stats = jnp.concatenate([peak_hi.T, peak_lo.T, denom_hi.T, denom_lo.T], axis=1)
    parcel = jnp.concatenate([part.reshape(row_rows, node_width), stats], axis=1).astype(BF16)
    share = row_rows // cols_n
    heard = lax.all_to_all(
        parcel.reshape(cols_n, share, parcel.shape[1]), "col", 0, 0, tiled=True
    ).astype(F32)
    tail = [
        heard[:, :, node_width + k * heads : node_width + (k + 1) * heads] for k in range(4)
    ]
    peaks = tail[0] + tail[1]
    factor = jnp.exp(peaks - jnp.max(peaks, axis=0, keepdims=True))
    total = jnp.sum(factor * (tail[2] + tail[3]), axis=0)
    mixed = jnp.sum(
        heard[:, :, :node_width].reshape(cols_n, share, heads, head_size) * factor[..., None], axis=0
    )
    attended = (mixed / total[..., None]).reshape(share, node_width).astype(BF16)
    everyone = lax.all_to_all(
        jnp.broadcast_to(attended[None], (cols_n,) + attended.shape), "col", 0, 0, tiled=True
    )
    node_update = jnp.dot(
        everyone.reshape(row_rows, node_width), w_out, preferred_element_type=F32
    ).astype(BF16)

    def edge_mlp(start, zed_back):
        zed_here = lax.dynamic_slice_in_dim(zed, start, key_cols, 0)
        pair_here = lax.dynamic_slice_in_dim(pair, start, key_cols, 0)
        joined = jnp.concatenate([zed_here, zed_back], axis=-1).reshape(-1, 2 * pair_width)
        hidden = jax.nn.gelu(jnp.dot(joined, w_in, preferred_element_type=F32) + b_in).astype(BF16)
        update = jnp.dot(hidden, w_mlp_out, preferred_element_type=F32) + b_out
        return (pair_here.astype(F32) + update.reshape(pair_here.shape)).astype(BF16)

    out = jnp.zeros(pair.shape, BF16)
    out = lax.dynamic_update_slice_in_dim(out, edge_mlp(odd * key_cols, back_one), odd * key_cols, 0)
    out = lax.dynamic_update_slice_in_dim(
        out, edge_mlp((1 - odd) * key_cols, back_two), (1 - odd) * key_cols, 0
    )
    return (node_update, out)


def solution(mesh):
    return jax.shard_map(
        body,
        mesh=mesh,
        in_specs=(
            P("col", None),
            P(),
            P(None, None, "row"),
            P(None, "col"),
            P("row", "col", None),
            P(),
            P(),
            P(),
            P(),
            P(),
            P(),
            P(),
            P(),
        ),
        out_specs=(P("row", "col"), P("row", "col", None)),
        check_vma=False,
    )
```

time: 392 us -> 117 us (0.30)
  the two profiles are of different devices: /device:TPU:1 before, /device:TPU:129 now
where the time goes in v1:
time: 117 us; the launch traced here: 116 us
  starting transfers between devices  55.7 us (48%)
  waiting for transfers between devices  40 us (34%)
  local copies, waits for them, and re-layouts  7.37 us (6%)
  other arithmetic  6.29 us (5%)
  matrix products  6 us (5%)
    all_to_all x1, waiting for transfers between devices, body(): got = lax.all_to_all(sent, 'row', 0, 0, tiled=True)  25.6 us
    all_to_all x1, starting transfers between devices, body(): got = lax.all_to_all(sent, 'row', 0, 0, tiled=True)  21.9 us
    all_to_all x1, starting transfers between devices, body(): lax.all_to_all(parcel.reshape(cols_n, share, parcel.shape[1]), 'col', 0,...  12 us
    all_to_all x1, starting transfers between devices, body(): all_q = lax.all_to_all(spread, 'col', 0, 0, tiled=True)  9.19 us
    all_to_all x1, waiting for transfers between devices, body(): lax.all_to_all(jnp.broadcast_to(attended[None], (cols_n,) + attended.shap...  8.07 us
    ppermute x1, starting transfers between devices, body(): back_two = lax.ppermute(second, ('row', 'col'), swap)  6.76 us
    all_to_all x1, waiting for transfers between devices, body(): lax.all_to_all(parcel.reshape(cols_n, share, parcel.shape[1]), 'col', 0,...  6.36 us
    all_to_all x1, starting transfers between devices, body(): lax.all_to_all(jnp.broadcast_to(attended[None], (cols_n,) + attended.shap...  3.9 us
  transfers between devices with their start and end apart: 6, of which 3 were waited for; matrix products, arithmetic and copies ran while one was open for 10% of the time, Pallas kernels for 0%

profile of v1, /device:TPU:129, one launch (start us, length us, event | category | flops | bytes accessed | tf_op | source)
XLA Modules:
  0.0 116.5 jit_solution(8437839112001398695)
XLA Ops:
  0.7 1.0 convert_reduce_fusion.1
  1.6 1.0 fusion.48
  2.6 1.2 %fusion.24 = bf16[3,32,48]{2,1,0:T(8,128)(2,1)S(1)} fusion(bf16[3,768,48]{1,2,0:T(8,128)(2,1)} %param.15, bf16[32,768]{1,0:T(8,128)(2,1)} %param.13, f32[768]{0:T(1024)} %param.14, f32[32]{0:T(128)S(1)} %add_rsqrt_fusion.1, f32[32]{0:T(128)S(1)} %broadcast_multiply_fusion.1), kind=kOutput, calls=%fused_computation.31 | convolution fusion | flops 7205376 | bytes 282880 | tf_op jit(solution)/shard_map/nd,kde->kne/dot_general | solution.py:48
  4.0 0.7 broadcast_in_dim.11
  4.7 9.2 %all-to-all-start = ((bf16[32,16,96]{2,1,0:T(8,128)(2,1)}), bf16[32,16,96]{2,1,0:T(8,128)(2,1)S(1)}, u32[]{:S(2)}, u32[]{:S(2)}) async-start(bf16[32,16,96]{2,1,0:T(8,128)(2,1)} %broadcast_in_dim.11), calls=%async_computation | async-start | bytes 262144 | tf_op jit(solution)/shard_map/all_to_all | solution.py:51
  14.3 0.6 fusion.25
  15.7 1.9 %collective-permute-start = (bf16[32,32,128]{2,1,0:T(8,128)(2,1)S(1)}, bf16[32,32,128]{2,1,0:T(8,128)(2,1)S(1)}, u32[]{:S(2)}, u32[]{:S(2)}) collective-permute-start(bf16[32,32,128]{2,1,0:T(8,128)(2,1)S(1)} %bitcast.76), channel_id=1, source_target_pairs={{0,0},{1,1},{2,32},{3,33},{4,64},{5,65},{6,96},{7,97},{8,128},{9,1... | collective-permute-start | bytes 786440 | tf_op jit(solution)/shard_map/ppermute | solution.py:68
  17.6 0.8 copy.49
  18.4 6.8 %collective-permute-start.1 = (bf16[32,32,128]{2,1,0:T(8,128)(2,1)}, bf16[32,32,128]{2,1,0:T(8,128)(2,1)}, u32[]{:S(2)}, u32[]{:S(2)}) collective-permute-start(bf16[32,32,128]{2,1,0:T(8,128)(2,1)} %bitcast.64), channel_id=1, source_target_pairs={{0,1},{1,0},{2,33},{3,32},{4,65},{5,64},{6,97},{7,96},{8,129},{9,1... | collective-permute-start | bytes 786440 | tf_op jit(solution)/shard_map/ppermute | solution.py:69
  25.3 0.8 pad_maximum_fusion.2
  26.0 21.9 %all-to-all-start.1 = ((bf16[16,64,96]{2,1,0:T(8,128)(2,1)}), bf16[16,64,96]{2,1,0:T(8,128)(2,1)S(1)}, u32[]{:S(2)}, u32[]{:S(2)}) async-start(bf16[16,64,96]{2,1,0:T(8,128)(2,1)} %pad_maximum_fusion.2), calls=%async_computation.1 | async-start | bytes 524288 | tf_op jit(solution)/shard_map/all_to_all | solution.py:79
  48.0 0.8 fusion.68
  50.1 0.8 copy-done.7
  50.9 1.1 fusion.20
  52.0 25.6 %all-to-all-done.1 = bf16[16,64,96]{2,1,0:T(8,128)(2,1)S(1)} async-done(((bf16[16,64,96]{2,1,0:T(8,128)(2,1)}), bf16[16,64,96]{2,1,0:T(8,128)(2,1)S(1)}, u32[]{:S(2)}, u32[]{:S(2)}) %all-to-all-start.1) | async-done | bytes 196640 | tf_op jit(solution)/shard_map/all_to_all | solution.py:79
  80.0 1.0 concatenate.38
  81.0 12.0 %all-to-all-start.2 = ((bf16[32,2,832]{2,1,0:T(2,128)(2,1)}), bf16[32,2,832]{2,1,0:T(2,128)(2,1)S(1)}, u32[]{:S(2)}, u32[]{:S(2)}) async-start(bf16[32,2,832]{2,1,0:T(2,128)(2,1)} %concatenate.38), calls=%async_computation.2 | async-start | bytes 229376 | tf_op jit(solution)/shard_map/all_to_all | solution.py:107
  93.0 1.0 pad_maximum_fusion.1
  94.0 1.1 fusion.21
  95.1 6.4 %all-to-all-done.2 = bf16[32,2,832]{2,1,0:T(2,128)(2,1)S(1)} async-done(((bf16[32,2,832]{2,1,0:T(2,128)(2,1)}), bf16[32,2,832]{2,1,0:T(2,128)(2,1)S(1)}, u32[]{:S(2)}, u32[]{:S(2)}) %all-to-all-start.2) | async-done | bytes 106528 | tf_op jit(solution)/shard_map/all_to_all | solution.py:107
  102.7 0.7 broadcast_in_dim.13
  103.4 3.9 %all-to-all-start.3 = ((bf16[32,2,768]{2,1,0:T(2,128)(2,1)}), bf16[32,2,768]{2,1,0:T(2,128)(2,1)S(1)}, u32[]{:S(2)}, u32[]{:S(2)}) async-start(bf16[32,2,768]{2,1,0:T(2,128)(2,1)} %broadcast_in_dim.13), calls=%async_computation.3 | async-start | bytes 196608 | tf_op jit(solution)/shard_map/all_to_all | solution.py:120
  107.6 8.1 %all-to-all-done.3 = bf16[32,2,768]{2,1,0:T(2,128)(2,1)S(1)} async-done(((bf16[32,2,768]{2,1,0:T(2,128)(2,1)}), bf16[32,2,768]{2,1,0:T(2,128)(2,1)S(1)}, u32[]{:S(2)}, u32[]{:S(2)}) %all-to-all-start.3) | async-done | bytes 98336 | tf_op jit(solution)/shard_map/all_to_all | solution.py:120
  115.7 0.7 convolution_convert_fusion.2
  (72 shorter events, 6.4 us)
Async XLA Ops:
  0.6 49.5 %copy-start = (bf16[256,512]{1,0:T(8,128)(2,1)S(1)}, bf16[256,512]{1,0:T(8,128)(2,1)}, u32[]{:S(2)}) copy-start(bf16[256,512]{1,0:T(8,128)(2,1)} %param.22) | copy-start | bytes 786436
  0.6 13.2 %copy-start.1 = (bf16[64,32,128]{2,1,0:T(8,128)(2,1)S(1)}, bf16[64,32,128]{2,1,0:T(8,128)(2,1)}, u32[]{:S(2)}) copy-start(bf16[64,32,128]{2,1,0:T(8,128)(2,1)} %param.17) | copy-start | bytes 1572868
  4.7 20.6 %all-to-all-start = ((bf16[32,16,96]{2,1,0:T(8,128)(2,1)}), bf16[32,16,96]{2,1,0:T(8,128)(2,1)S(1)}, u32[]{:S(2)}, u32[]{:S(2)}) async-start(bf16[32,16,96]{2,1,0:T(8,128)(2,1)} %broadcast_in_dim.11), calls=%async_computation | async-start | bytes 262144 | tf_op jit(solution)/shard_map/all_to_all | solution.py:51
  13.9 1.0 copy-start.6
  15.7 34.3 %collective-permute-start = (bf16[32,32,128]{2,1,0:T(8,128)(2,1)S(1)}, bf16[32,32,128]{2,1,0:T(8,128)(2,1)S(1)}, u32[]{:S(2)}, u32[]{:S(2)}) collective-permute-start(bf16[32,32,128]{2,1,0:T(8,128)(2,1)S(1)} %bitcast.76), channel_id=1, source_target_pairs={{0,0},{1,1},{2,32},{3,33},{4,64},{5,65},{6,96},{7,97},{8,128},{9,1... | collective-permute-start | bytes 786440 | tf_op jit(solution)/shard_map/ppermute | solution.py:68
  18.4 74.6 %collective-permute-start.1 = (bf16[32,32,128]{2,1,0:T(8,128)(2,1)}, bf16[32,32,128]{2,1,0:T(8,128)(2,1)}, u32[]{:S(2)}, u32[]{:S(2)}) collective-permute-start(bf16[32,32,128]{2,1,0:T(8,128)(2,1)} %bitcast.64), channel_id=1, source_target_pairs={{0,1},{1,0},{2,33},{3,32},{4,65},{5,64},{6,97},{7,96},{8,129},{9,1... | collective-permute-start | bytes 786440 | tf_op jit(solution)/shard_map/ppermute | solution.py:69
  25.3 22.7 %copy-start.4 = (bf16[128,16]{0,1:T(8,128)(2,1)S(1)}, bf16[128,16]{0,1:T(8,128)(2,1)}, u32[]{:S(2)}) copy-start(bf16[128,16]{0,1:T(8,128)(2,1)} %param.20) | copy-start | bytes 12292
  26.0 51.5 %all-to-all-start.1 = ((bf16[16,64,96]{2,1,0:T(8,128)(2,1)}), bf16[16,64,96]{2,1,0:T(8,128)(2,1)S(1)}, u32[]{:S(2)}, u32[]{:S(2)}) async-start(bf16[16,64,96]{2,1,0:T(8,128)(2,1)} %pad_maximum_fusion.2), calls=%async_computation.1 | async-start | bytes 524288 | tf_op jit(solution)/shard_map/all_to_all | solution.py:79
  48.8 0.7 copy-start.5
  50.0 0.9 copy-start.7
  50.0 0.9 copy-start.8
  50.0 0.9 copy-start.10
  77.9 0.7 copy-start.9
  81.0 20.5 %all-to-all-start.2 = ((bf16[32,2,832]{2,1,0:T(2,128)(2,1)}), bf16[32,2,832]{2,1,0:T(2,128)(2,1)S(1)}, u32[]{:S(2)}, u32[]{:S(2)}) async-start(bf16[32,2,832]{2,1,0:T(2,128)(2,1)} %concatenate.38), calls=%async_computation.2 | async-start | bytes 229376 | tf_op jit(solution)/shard_map/all_to_all | solution.py:107
  103.4 12.3 %all-to-all-start.3 = ((bf16[32,2,768]{2,1,0:T(2,128)(2,1)}), bf16[32,2,768]{2,1,0:T(2,128)(2,1)S(1)}, u32[]{:S(2)}, u32[]{:S(2)}) async-start(bf16[32,2,768]{2,1,0:T(2,128)(2,1)} %broadcast_in_dim.13), calls=%async_computation.3 | async-start | bytes 196608 | tf_op jit(solution)/shard_map/all_to_all | solution.py:120
  107.5 8.2 %copy-start.3 = (bf16[768,24]{0,1:T(8,128)(2,1)S(1)}, bf16[768,24]{0,1:T(8,128)(2,1)}, u32[]{:S(2)}) copy-start(bf16[768,24]{0,1:T(8,128)(2,1)} %param.16) | copy-start | bytes 110596
  107.6 8.9 %copy-start.2 = (bf16[64,32,128]{2,1,0:T(8,128)(2,1)}, bf16[64,32,128]{2,1,0:T(8,128)(2,1)S(1)}, u32[]{:S(2)}) copy-start(bf16[64,32,128]{2,1,0:T(8,128)(2,1)S(1)} %fusion.41) | copy-start | bytes 1572868

commit v2 on v1

v2 whole, which is shorter than its diff:
```python
import math

import jax
import jax.numpy as jnp
from jax import lax
from jax.sharding import PartitionSpec as P

F32 = jnp.float32
BF16 = jnp.bfloat16
PLAN = [('a', 0, 2, 'att'), ('a', 1, 2, 'att'), ('b', 0, 2, 'att'), ('b', 1, 2, 'end')]
LONG = ("row", "col")


def tie(value, *others):
    return lax.optimization_barrier((value,) + others)[0]


def rounded(values):
    return lax.reduce_precision(values, 8, 7)


def layer_norm(values_in, scale_gain):
    centred = values_in.astype(F32)
    centred = centred - jnp.mean(centred, axis=-1, keepdims=True)
    variance = jnp.mean(centred * centred, axis=-1, keepdims=True)
    return centred * lax.rsqrt(variance + 1e-05) * scale_gain


def body(
    nodes, node_gain, w_qkv, w_out, pair, pair_gain, w_bias, w_gate, b_gate, w_in, b_in, w_mlp_out, b_out,
):
    rows_n = lax.axis_size("row")
    cols_n = lax.axis_size("col")
    key_rows, node_width = nodes.shape
    row_rows, key_cols, pair_width = pair.shape
    heads = w_bias.shape[1]
    head_size = node_width // heads
    half = key_rows // 2
    col = lax.axis_index("col")
    odd = col % 2
    same = [
        (r * cols_n + c, (c // 2) * cols_n + 2 * r + c % 2) for r in range(rows_n) for c in range(cols_n)
    ]
    swap = [
        (r * cols_n + c, (c // 2) * cols_n + 2 * r + 1 - c % 2) for r in range(rows_n) for c in range(cols_n)
    ]

    zed = layer_norm(pair, pair_gain).astype(BF16)
    landed = []
    for which, part, parts, late in PLAN:
        own = odd if which == "a" else 1 - odd
        rows = key_cols // parts
        tile = lax.dynamic_slice_in_dim(zed, own * key_cols, key_cols, 0)[:, part * rows : (part + 1) * rows]
        landed.append(
            (lax.ppermute(jnp.transpose(tile, (1, 0, 2)), LONG, same if which == "a" else swap), own * key_cols + part * rows, late)
        )
    normed = layer_norm(nodes, node_gain).astype(BF16)
    proj = jnp.einsum("nd,kde->kne", normed, w_qkv, preferred_element_type=F32).astype(BF16)
    packed = jnp.concatenate([proj[:, :half], proj[:, half:]], axis=-1)
    spread = jnp.broadcast_to(packed[0][None], (cols_n,) + packed.shape[1:])
    all_q = lax.all_to_all(spread, "col", 0, 0, tiled=True)
    blocks = all_q.reshape(rows_n, 2, half, 2 * head_size)
    own = [jnp.broadcast_to(packed[k][None], (rows_n,) + packed.shape[1:]) for k in (1, 2)]
    sent = jnp.concatenate([blocks[:, 0], blocks[:, 1]] + own, axis=-1)
    got = lax.all_to_all(sent, "row", 0, 0, tiled=True)

    def unpack(piece):
        chunks = piece.shape[2] // head_size
        piece = piece.reshape(heads, half, chunks, head_size)
        return jnp.transpose(piece, (0, 2, 1, 3)).reshape(heads, chunks * half, head_size)

    width = 2 * head_size
    query = unpack(got[:, :, : 2 * width])
    key = unpack(got[:, :, 2 * width : 3 * width])
    value = unpack(got[:, :, 3 * width :])

    scores = jnp.einsum("hie,hje->hij", query, key, preferred_element_type=F32) / math.sqrt(head_size)
    pair_bias = jnp.einsum("ijc,ch->hij", pair, w_bias, preferred_element_type=F32)
    gate_prob = jax.nn.sigmoid(
        jnp.einsum("ijc,ch->hij", zed, w_gate, preferred_element_type=F32) + b_gate[:, None, None]
    )
    logits = scores + pair_bias
    peak = jnp.max(logits, axis=2)
    peak_hi = rounded(peak)
    peak_lo = rounded(peak - peak_hi)
    expo = jnp.exp(logits - (peak_hi + peak_lo)[:, :, None])
    denom = jnp.sum(expo, axis=2)
    weights = (expo * gate_prob).astype(BF16)
    part = jnp.einsum("hij,hje->ihe", weights, value, preferred_element_type=F32)
    denom_hi = rounded(denom)
    denom_lo = rounded(denom - denom_hi)
    stats = jnp.concatenate([peak_hi.T, peak_lo.T, denom_hi.T, denom_lo.T], axis=1)
    parcel = jnp.concatenate([part.reshape(row_rows, node_width), stats], axis=1).astype(BF16)
    share = row_rows // cols_n
    heard = lax.all_to_all(parcel.reshape(cols_n, share, parcel.shape[1]), "col", 0, 0, tiled=True)
    heard = heard.astype(F32)
    tail = [heard[:, :, node_width + k * heads : node_width + (k + 1) * heads] for k in range(4)]
    peaks = tail[0] + tail[1]
    factor = jnp.exp(peaks - jnp.max(peaks, axis=0, keepdims=True))
    total = jnp.sum(factor * (tail[2] + tail[3]), axis=0)
    mixed = jnp.sum(
        heard[:, :, :node_width].reshape(cols_n, share, heads, head_size) * factor[..., None], axis=0
    )
    attended = (mixed / total[..., None]).reshape(share, node_width).astype(BF16)
    everyone = lax.all_to_all(
        jnp.broadcast_to(attended[None], (cols_n,) + attended.shape), "col", 0, 0, tiled=True
    )
    node_update = jnp.dot(
        everyone.reshape(row_rows, node_width), w_out, preferred_element_type=F32
    ).astype(BF16)

    def edge_mlp(start, zed_back):
        count = zed_back.shape[0]
        zed_here = lax.dynamic_slice_in_dim(zed, start, count, 0)
        pair_here = lax.dynamic_slice_in_dim(pair, start, count, 0)
        joined = jnp.concatenate([zed_here, zed_back], axis=-1).reshape(-1, 2 * pair_width)
        hidden = jax.nn.gelu(jnp.dot(joined, w_in, preferred_element_type=F32) + b_in).astype(BF16)
        update = jnp.dot(hidden, w_mlp_out, preferred_element_type=F32) + b_out
        return (pair_here.astype(F32) + update.reshape(pair_here.shape)).astype(BF16)

    out = jnp.zeros(pair.shape, BF16)
    for back, start, late in landed:
        back = tie(back, attended if late == "att" else everyone)
        out = lax.dynamic_update_slice_in_dim(out, edge_mlp(start, back), start, 0)
    return (node_update, out)


def solution(mesh):
    return jax.shard_map(
        body,
        mesh=mesh,
        in_specs=(
            P("col", None), P(), P(None, None, "row"), P(None, "col"), P("row", "col", None),
            P(), P(), P(), P(), P(), P(), P(), P(),
        ),
        out_specs=(P("row", "col"), P("row", "col", None)),
        check_vma=False,
    )
```

time: 117 us -> 123 us (1.051)
  the two profiles are of different devices: /device:TPU:129 before, /device:TPU:1 now
where the time goes in v2:
time: 123 us
  starting transfers between devices  73.4 us (60%)
  waiting for transfers between devices  29 us (24%)
  local copies, waits for them, and re-layouts  8.03 us (7%)
  matrix products  6.5 us (5%)
  other arithmetic  4.61 us (4%)
    all_to_all x1, starting transfers between devices, body(): lax.all_to_all(jnp.broadcast_to(attended[None], (cols_n,) + attended.shap...  33.8 us
    all_to_all x1, starting transfers between devices, body(): got = lax.all_to_all(sent, 'row', 0, 0, tiled=True)  14.5 us
    all_to_all x1, waiting for transfers between devices, body(): got = lax.all_to_all(sent, 'row', 0, 0, tiled=True)  13 us
    all_to_all x1, starting transfers between devices, body(): all_q = lax.all_to_all(spread, 'col', 0, 0, tiled=True)  10.3 us
    all_to_all x1, starting transfers between devices, body(): lax.all_to_all(parcel.reshape(cols_n, share, parcel.shape[1]), 'col', 0,...  9.04 us
    all_to_all x1, waiting for transfers between devices, body(): all_q = lax.all_to_all(spread, 'col', 0, 0, tiled=True)  7.77 us
    all_to_all x1, waiting for transfers between devices, body(): lax.all_to_all(jnp.broadcast_to(attended[None], (cols_n,) + attended.shap...  5.78 us
    ppermute x4, starting transfers between devices, body(): lax.ppermute(jnp.transpose(tile, (1, 0, 2)), LONG, same if which == 'a' e...  5.66 us
  transfers between devices with their start and end apart: 8, of which 4 were waited for; matrix products, arithmetic and copies ran while one was open for 6% of the time, Pallas kernels for 0%

profile of v2, /device:TPU:1, one launch (start us, length us, event | category | flops | bytes accessed | tf_op | source)
XLA Modules:
  0.0 122.7 jit_solution(3304328081465898334)
XLA Ops:
  0.7 1.0 convert_reduce_fusion.1
  1.9 1.2 fusion.4
  3.2 0.7 broadcast_in_dim.17
  3.9 10.3 %all-to-all-start = ((bf16[32,16,96]{2,1,0:T(8,128)(2,1)}), bf16[32,16,96]{2,1,0:T(8,128)(2,1)S(1)}, u32[]{:S(2)}, u32[]{:S(2)}) async-start(bf16[32,16,96]{2,1,0:T(8,128)(2,1)} %broadcast_in_dim.17), calls=%async_computation | async-start | bytes 262144 | tf_op jit(solution)/shard_map/all_to_all | solution.py:61
  15.2 7.8 %all-to-all-done = bf16[32,16,96]{2,1,0:T(8,128)(2,1)S(1)} async-done(((bf16[32,16,96]{2,1,0:T(8,128)(2,1)}), bf16[32,16,96]{2,1,0:T(8,128)(2,1)S(1)}, u32[]{:S(2)}, u32[]{:S(2)}) %all-to-all-start) | async-done | bytes 98336 | tf_op jit(solution)/shard_map/all_to_all | solution.py:61
  23.1 0.8 pad_maximum_fusion.4
  23.9 14.5 %all-to-all-start.1 = ((bf16[16,16,384]{2,1,0:T(8,128)(2,1)}), bf16[16,16,384]{2,1,0:T(8,128)(2,1)S(1)}, u32[]{:S(2)}, u32[]{:S(2)}) async-start(bf16[16,16,384]{2,1,0:T(8,128)(2,1)} %pad_maximum_fusion.4), calls=%async_computation.1 | async-start | bytes 393216 | tf_op jit(solution)/shard_map/all_to_all | solution.py:65
  39.1 0.8 fusion.92
  41.1 13.0 %all-to-all-done.1 = bf16[16,16,384]{2,1,0:T(8,128)(2,1)S(1)} async-done(((bf16[16,16,384]{2,1,0:T(8,128)(2,1)}), bf16[16,16,384]{2,1,0:T(8,128)(2,1)S(1)}, u32[]{:S(2)}, u32[]{:S(2)}) %all-to-all-start.1) | async-done | bytes 196640 | tf_op jit(solution)/shard_map/all_to_all | solution.py:65
  57.1 1.0 concatenate.40
  58.1 9.0 %all-to-all-start.2 = ((bf16[32,2,832]{2,1,0:T(2,128)(2,1)}), bf16[32,2,832]{2,1,0:T(2,128)(2,1)S(1)}, u32[]{:S(2)}, u32[]{:S(2)}) async-start(bf16[32,2,832]{2,1,0:T(2,128)(2,1)} %concatenate.40), calls=%async_computation.2 | async-start | bytes 229376 | tf_op jit(solution)/shard_map/all_to_all | solution.py:95
  67.3 2.1 %collective-permute-start.3 = (bf16[16,32,128]{2,1,0:T(8,128)(2,1)S(1)}, bf16[16,32,128]{2,1,0:T(8,128)(2,1)S(1)}, u32[]{:S(2)}, u32[]{:S(2)}) collective-permute-start(bf16[16,32,128]{2,1,0:T(8,128)(2,1)S(1)} %bitcast.102), channel_id=1, source_target_pairs={{0,1},{1,0},{2,33},{3,32},{4,65},{5,64},{6,97},{7,96},{8,129},{9,1... | collective-permute-start | bytes 393224 | tf_op jit(solution)/shard_map/ppermute | solution.py:55
  69.5 2.2 %collective-permute-start.2 = (bf16[16,32,128]{2,1,0:T(8,128)(2,1)S(1)}, bf16[16,32,128]{2,1,0:T(8,128)(2,1)S(1)}, u32[]{:S(2)}, u32[]{:S(2)}) collective-permute-start(bf16[16,32,128]{2,1,0:T(8,128)(2,1)S(1)} %bitcast.103), channel_id=1, source_target_pairs={{0,1},{1,0},{2,33},{3,32},{4,65},{5,64},{6,97},{7,96},{8,129},{9,1... | collective-permute-start | bytes 393224 | tf_op jit(solution)/shard_map/ppermute | solution.py:55
  71.7 0.7 collective-permute-start.1
  72.4 0.7 collective-permute-start
  73.2 2.5 %all-to-all-done.2 = bf16[32,2,832]{2,1,0:T(2,128)(2,1)S(1)} async-done(((bf16[32,2,832]{2,1,0:T(2,128)(2,1)}), bf16[32,2,832]{2,1,0:T(2,128)(2,1)S(1)}, u32[]{:S(2)}, u32[]{:S(2)}) %all-to-all-start.2) | async-done | bytes 106528 | tf_op jit(solution)/shard_map/all_to_all | solution.py:95
  76.9 0.7 broadcast_in_dim.22
  77.6 33.8 %all-to-all-start.3 = ((bf16[32,2,768]{2,1,0:T(2,128)(2,1)}), bf16[32,2,768]{2,1,0:T(2,128)(2,1)S(1)}, u32[]{:S(2)}, u32[]{:S(2)}) async-start(bf16[32,2,768]{2,1,0:T(2,128)(2,1)} %broadcast_in_dim.22), calls=%async_computation.3 | async-start | bytes 196608 | tf_op jit(solution)/shard_map/all_to_all | solution.py:105
  111.5 0.8 copy-done.8
  113.0 0.7 convolution_add_fusion.6
  113.9 5.8 %all-to-all-done.3 = bf16[32,2,768]{2,1,0:T(2,128)(2,1)S(1)} async-done(((bf16[32,2,768]{2,1,0:T(2,128)(2,1)}), bf16[32,2,768]{2,1,0:T(2,128)(2,1)S(1)}, u32[]{:S(2)}, u32[]{:S(2)}) %all-to-all-start.3) | async-done | bytes 98336 | tf_op jit(solution)/shard_map/all_to_all | solution.py:105
  120.4 0.7 convolution_add_fusion.4
  121.2 0.7 copy-done.4
  122.0 0.7 convolution_convert_fusion.2
  (86 shorter events, 9.4 us)
Async XLA Ops:
  0.6 110.9 %copy-start = (bf16[256,512]{1,0:T(8,128)(2,1)S(1)}, bf16[256,512]{1,0:T(8,128)(2,1)}, u32[]{:S(2)}) copy-start(bf16[256,512]{1,0:T(8,128)(2,1)} %param.22) | copy-start | bytes 786436
  0.6 1.0 copy-start.3
  0.7 13.6 %copy-start.1 = (bf16[64,32,128]{2,1,0:T(8,128)(2,1)S(1)}, bf16[64,32,128]{2,1,0:T(8,128)(2,1)}, u32[]{:S(2)}) copy-start(bf16[64,32,128]{2,1,0:T(8,128)(2,1)} %param.17) | copy-start | bytes 1572868
  3.9 19.2 %all-to-all-start = ((bf16[32,16,96]{2,1,0:T(8,128)(2,1)}), bf16[32,16,96]{2,1,0:T(8,128)(2,1)S(1)}, u32[]{:S(2)}, u32[]{:S(2)}) async-start(bf16[32,16,96]{2,1,0:T(8,128)(2,1)} %broadcast_in_dim.17), calls=%async_computation | async-start | bytes 262144 | tf_op jit(solution)/shard_map/all_to_all | solution.py:61
  23.9 14.5 %copy-start.7 = (f32[128]{0:T(128)S(1)}, f32[128]{0:T(128)}, u32[]{:S(2)}) copy-start(f32[128]{0:T(128)} %param.18) | copy-start | bytes 1540
  23.9 30.2 %all-to-all-start.1 = ((bf16[16,16,384]{2,1,0:T(8,128)(2,1)}), bf16[16,16,384]{2,1,0:T(8,128)(2,1)S(1)}, u32[]{:S(2)}, u32[]{:S(2)}) async-start(bf16[16,16,384]{2,1,0:T(8,128)(2,1)} %pad_maximum_fusion.4), calls=%async_computation.1 | async-start | bytes 393216 | tf_op jit(solution)/shard_map/all_to_all | solution.py:65
  38.4 0.7 copy-start.5
  39.9 0.7 copy-start.6
  55.1 0.7 copy-start.10
  58.1 17.5 %all-to-all-start.2 = ((bf16[32,2,832]{2,1,0:T(2,128)(2,1)}), bf16[32,2,832]{2,1,0:T(2,128)(2,1)S(1)}, u32[]{:S(2)}, u32[]{:S(2)}) async-start(bf16[32,2,832]{2,1,0:T(2,128)(2,1)} %concatenate.40), calls=%async_computation.2 | async-start | bytes 229376 | tf_op jit(solution)/shard_map/all_to_all | solution.py:95
  67.3 46.6 %collective-permute-start.3 = (bf16[16,32,128]{2,1,0:T(8,128)(2,1)S(1)}, bf16[16,32,128]{2,1,0:T(8,128)(2,1)S(1)}, u32[]{:S(2)}, u32[]{:S(2)}) collective-permute-start(bf16[16,32,128]{2,1,0:T(8,128)(2,1)S(1)} %bitcast.102), channel_id=1, source_target_pairs={{0,1},{1,0},{2,33},{3,32},{4,65},{5,64},{6,97},{7,96},{8,129},{9,1... | collective-permute-start | bytes 393224 | tf_op jit(solution)/shard_map/ppermute | solution.py:55
  69.5 41.9 %collective-permute-start.2 = (bf16[16,32,128]{2,1,0:T(8,128)(2,1)S(1)}, bf16[16,32,128]{2,1,0:T(8,128)(2,1)S(1)}, u32[]{:S(2)}, u32[]{:S(2)}) collective-permute-start(bf16[16,32,128]{2,1,0:T(8,128)(2,1)S(1)} %bitcast.103), channel_id=1, source_target_pairs={{0,1},{1,0},{2,33},{3,32},{4,65},{5,64},{6,97},{7,96},{8,129},{9,1... | collective-permute-start | bytes 393224 | tf_op jit(solution)/shard_map/ppermute | solution.py:55
  71.7 39.7 %collective-permute-start.1 = (bf16[16,32,128]{2,1,0:T(8,128)(2,1)S(1)}, bf16[16,32,128]{2,1,0:T(8,128)(2,1)S(1)}, u32[]{:S(2)}, u32[]{:S(2)}) collective-permute-start(bf16[16,32,128]{2,1,0:T(8,128)(2,1)S(1)} %bitcast.104), channel_id=1, source_target_pairs={{0,0},{1,1},{2,32},{3,33},{4,64},{5,65},{6,96},{7,97},{8,128},{9,1... | collective-permute-start | bytes 393224 | tf_op jit(solution)/shard_map/ppermute | solution.py:55
  72.4 39.0 %collective-permute-start = (bf16[16,32,128]{2,1,0:T(8,128)(2,1)S(1)}, bf16[16,32,128]{2,1,0:T(8,128)(2,1)S(1)}, u32[]{:S(2)}, u32[]{:S(2)}) collective-permute-start(bf16[16,32,128]{2,1,0:T(8,128)(2,1)S(1)} %bitcast.105), channel_id=1, source_target_pairs={{0,0},{1,1},{2,32},{3,33},{4,64},{5,65},{6,96},{7,97},{8,128},{9,1... | collective-permute-start | bytes 393224 | tf_op jit(solution)/shard_map/ppermute | solution.py:55
  77.6 42.1 %all-to-all-start.3 = ((bf16[32,2,768]{2,1,0:T(2,128)(2,1)}), bf16[32,2,768]{2,1,0:T(2,128)(2,1)S(1)}, u32[]{:S(2)}, u32[]{:S(2)}) async-start(bf16[32,2,768]{2,1,0:T(2,128)(2,1)} %broadcast_in_dim.22), calls=%async_computation.3 | async-start | bytes 196608 | tf_op jit(solution)/shard_map/all_to_all | solution.py:105
  111.4 0.9 copy-start.8
  111.5 0.8 copy-start.9
  111.5 0.8 copy-start.11
  121.1 1.6 %copy-start.2 = (bf16[64,32,128]{2,1,0:T(8,128)(2,1)}, bf16[64,32,128]{2,1,0:T(8,128)(2,1)S(1)}, u32[]{:S(2)}) copy-start(bf16[64,32,128]{2,1,0:T(8,128)(2,1)S(1)} %fusion.68) | copy-start | bytes 1572868
  121.2 0.8 copy-start.4

commit v3 on v2

v3 whole, which is shorter than its diff:
```python
import functools
import math

import jax
import jax.numpy as jnp
from jax import lax
from jax.experimental import pallas as pl
from jax.experimental.pallas import tpu as pltpu
from jax.sharding import PartitionSpec as P

F32 = jnp.float32
BF16 = jnp.bfloat16
LONG = ("row", "col")
LANES = 128
VMEM_BYTES = 20 << 20


def tie(value, *others):
    return lax.optimization_barrier((value,) + others)[0]


def layer_norm(values_in, scale_gain):
    centred = values_in.astype(F32)
    centred = centred - jnp.mean(centred, axis=-1, keepdims=True)
    variance = jnp.mean(centred * centred, axis=-1, keepdims=True)
    return centred * lax.rsqrt(variance + 1e-05) * scale_gain


def nt_dot(left, right):
    return lax.dot_general(left, right, (((1,), (1,)), ((), ())), preferred_element_type=F32)


def rounded(values):
    return values.astype(BF16).astype(F32)


def project_kernel(nodes_ref, gain_ref, w_ref, spread_ref, own_ref):
    normed = layer_norm(nodes_ref[...], gain_ref[...]).astype(BF16)
    half = normed.shape[0] // 2
    for which in range(3):
        proj = nt_dot(normed, w_ref[which])
        packed = jnp.concatenate([proj[:half], proj[half:]], axis=-1).astype(BF16)
        if which == 0:
            spread_ref[...] = jnp.broadcast_to(packed[None], spread_ref.shape)
        else:
            own_ref[which - 1] = packed


def attend_kernel(got_ref, bias_ref, gate_ref, select_ref, parcel_ref, *, heads, size):
    half = got_ref.shape[1]
    pairs = heads // 2
    width = pairs * LANES
    got = got_ref[...].astype(F32)
    blank = jnp.zeros((half, LANES - 2 * size), F32)

    def rows(chunk):
        cut = slice(chunk * size, (chunk + 1) * size)
        parts = []
        for p in range(pairs):
            parts += [got[2 * p][:, cut], got[2 * p + 1][:, cut], blank]
        return jnp.concatenate(parts, axis=-1)

    query = jnp.concatenate([rows(k) for k in range(4)], axis=0).astype(BF16)
    lane = lax.broadcasted_iota(jnp.int32, (heads, width), 1)
    head = lax.broadcasted_iota(jnp.int32, (heads, width), 0)
    inner = lane % LANES
    owner = jnp.where(inner < size, 2 * (lane // LANES), 2 * (lane // LANES) + 1)
    mask = jnp.where((owner == head) & (inner < 2 * size), 1.0, 0.0).astype(F32)

    def spread(first):
        flat = jnp.concatenate([rows(first), rows(first + 1)], axis=0)
        wide = jnp.broadcast_to(flat[:, None, :], (flat.shape[0], heads, width)) * mask[None]
        return wide.reshape(flat.shape[0] * heads, width).astype(BF16)

    logits = nt_dot(query, spread(4)) * (1.0 / math.sqrt(size)) + bias_ref[...]
    slabs = logits.shape[1] // LANES

    def over_keys(values, op):
        out = functools.reduce(op, [values[:, k * LANES : (k + 1) * LANES] for k in range(slabs)])
        step = heads
        while step < LANES:
            out = op(out, pltpu.roll(out, step, 1))
            step *= 2
        return out

    peak = over_keys(logits, jnp.maximum)
    peak_hi = rounded(peak)
    peak_lo = rounded(peak - peak_hi)
    expo = jnp.exp(logits - jnp.concatenate([peak_hi + peak_lo] * slabs, axis=-1))
    denom = over_keys(expo, jnp.add)
    denom_hi = rounded(denom)
    denom_lo = rounded(denom - denom_hi)
    part = jnp.dot((expo * gate_ref[...]).astype(BF16), spread(6), preferred_element_type=F32)
    at = lax.broadcasted_iota(jnp.int32, peak.shape, 1) // heads
    stats = jnp.where(at == 0, peak_hi, jnp.where(at == 1, peak_lo, jnp.where(at == 2, denom_hi, denom_lo)))
    stats = jnp.where(at < 4, stats, 0.0).astype(BF16)
    parcel = (part + jnp.dot(stats, select_ref[...], preferred_element_type=F32)).astype(BF16)
    groups = parcel.shape[0] // half
    for g in range(groups):
        for p in range(pairs):
            parcel_ref[g * pairs + p] = parcel[g * half : (g + 1) * half, p * LANES : (p + 1) * LANES]


def settle_kernel(heard_ref, out_ref, *, size):
    heard = heard_ref[...].astype(F32)
    base = 2 * size
    lane = lax.broadcasted_iota(jnp.int32, heard.shape[1:], 1)

    def stat(which, head):
        at = base + 2 * which + head
        return heard[:, :, at : at + 1]

    mixed = None
    factors, totals = [], []
    for head in range(2):
        peaks = stat(0, head) + stat(1, head)
        factor = jnp.exp(peaks - jnp.max(peaks, axis=0, keepdims=True))
        totals.append(jnp.sum(factor * (stat(2, head) + stat(3, head)), axis=0))
        factors.append(factor)
    first = (lane < size)[None]
    factor = jnp.where(first, factors[0], factors[1])
    mixed = jnp.sum(heard * factor, axis=0)
    total = jnp.where(lane < size, totals[0], totals[1])
    attended = jnp.where(lane < base, mixed / total, 0.0).astype(BF16)
    out_ref[...] = jnp.broadcast_to(attended[None], out_ref.shape)


def output_kernel(all_ref, w_ref, out_ref, *, pairs):
    groups = all_ref.shape[0] // pairs
    whole = jnp.concatenate(
        [jnp.concatenate([all_ref[g * pairs + p] for p in range(pairs)], axis=-1) for g in range(groups)], axis=0
    )
    out_ref[...] = nt_dot(w_ref[...], whole).astype(BF16)


def mlp_kernel(odd_ref, zed_ref, pair_ref, *refs):
    backs, (w_in_ref, b_in_ref, w_out_ref, b_out_ref, out_ref, here_ref) = refs[:4], refs[4:]
    for k in range(4):

        @pl.when(pl.program_id(0) == k)
        def _():
            here_ref[...] = backs[k][...]

    width = zed_ref.shape[2]
    joined = jnp.concatenate(
        [zed_ref[...].reshape(-1, width), here_ref[...].reshape(-1, width)], axis=-1
    )
    hidden = jax.nn.gelu(jnp.dot(joined, w_in_ref[...], preferred_element_type=F32) + b_in_ref[...]).astype(BF16)
    update = jnp.dot(hidden, w_out_ref[...], preferred_element_type=F32) + b_out_ref[...]
    out_ref[...] = (pair_ref[...].astype(F32) + update.reshape(pair_ref.shape)).astype(BF16)


def whole(kernel, out_shape, flops=1 << 20, moved=1 << 18):
    return pl.pallas_call(
        kernel, out_shape=out_shape,
        compiler_params=pltpu.CompilerParams(vmem_limit_bytes=VMEM_BYTES),
        cost_estimate=pl.CostEstimate(flops=flops, bytes_accessed=moved, transcendentals=0),
    )


PIECES = (("a", 0), ("a", 1), ("b", 0), ("b", 1))


def body(
    nodes, node_gain, w_qkv, w_out, pair, pair_gain, w_bias, w_gate, b_gate, w_in, b_in, w_mlp_out, b_out,
):
    rows_n = lax.axis_size("row")
    cols_n = lax.axis_size("col")
    key_rows, node_width = nodes.shape
    row_rows, key_cols, pair_width = pair.shape
    heads = w_bias.shape[1]
    size = node_width // heads
    half = key_rows // 2
    pairs = heads // 2
    hidden_width = w_in.shape[1]
    odd = lax.axis_index("col") % 2
    ends = [(r * cols_n + c, (c // 2) * cols_n + 2 * r) for r in range(rows_n) for c in range(cols_n)]
    same = [(source, base + source % 2) for source, base in ends]
    swap = [(source, base + 1 - source % 2) for source, base in ends]

    spread, own = whole(
        project_kernel,
        (
            jax.ShapeDtypeStruct((cols_n, half, 2 * size), BF16),
            jax.ShapeDtypeStruct((2, half, 2 * size), BF16),
        ),
    )(nodes, node_gain[None], jnp.transpose(w_qkv, (0, 2, 1)))
    all_q = lax.all_to_all(spread, "col", 0, 0, tiled=True)

    zed = layer_norm(tie(pair, own), pair_gain).astype(BF16)
    landed = []
    for which, part in PIECES:
        mine = odd if which == "a" else 1 - odd
        rows = key_cols // 2
        tile = lax.dynamic_slice_in_dim(zed, mine * key_cols, key_cols, 0)[:, part * rows : (part + 1) * rows]
        landed.append(lax.ppermute(jnp.transpose(tile, (1, 0, 2)), LONG, same if which == "a" else swap))

    blocks = all_q.reshape(rows_n, 2, half, 2 * size)
    mine = [jnp.broadcast_to(own[k][None], (rows_n, half, 2 * size)) for k in range(2)]
    sent = jnp.concatenate([blocks[:, 0], blocks[:, 1]] + mine, axis=-1)
    got = lax.all_to_all(sent, "row", 0, 0, tiled=True)

    pair_bias = jnp.einsum("ijc,ch->ijh", pair, w_bias, preferred_element_type=F32)
    gate_prob = jax.nn.sigmoid(jnp.einsum("ijc,ch->ijh", zed, w_gate, preferred_element_type=F32) + b_gate)
    flat = (row_rows, key_cols * heads)
    pair_bias, gate_prob = pair_bias.reshape(flat), gate_prob.reshape(flat)

    stat = jnp.arange(LANES)[:, None]
    place = jnp.arange(pairs * LANES)[None]
    target = (stat % heads) // 2 * LANES + 2 * size + 2 * (stat // heads) + stat % 2
    select = ((place == target) & (stat < 4 * heads)).astype(BF16)
    parcel = whole(
        functools.partial(attend_kernel, heads=heads, size=size),
        jax.ShapeDtypeStruct((cols_n, row_rows * pairs // cols_n, LANES), BF16),
    )(got, pair_bias, gate_prob, select)
    heard = lax.all_to_all(parcel, "col", 0, 0, tiled=True)
    settled = whole(functools.partial(settle_kernel, size=size), jax.ShapeDtypeStruct(parcel.shape, BF16))(heard)
    everyone = lax.all_to_all(settled, "col", 0, 0, tiled=True)

    w_wide = jnp.pad(
        w_out.T.reshape(w_out.shape[1], pairs, 2 * size), ((0, 0), (0, 0), (0, LANES - 2 * size))
    ).reshape(w_out.shape[1], pairs * LANES)
    node_update = whole(
        functools.partial(output_kernel, pairs=pairs), jax.ShapeDtypeStruct((w_out.shape[1], row_rows), BF16)
    )(everyone, w_wide).T

    landed = [tie(back, settled) for back in landed]
    block = key_cols // 2

    def tile_at(k, odd_ref):
        return (jnp.where(k < 2, odd_ref[0], 1 - odd_ref[0]) * 2 + k % 2, 0, 0)

    def fixed(*shape):
        return pl.BlockSpec(shape, lambda k, odd_ref: (0,) * len(shape))

    tile_spec = pl.BlockSpec((block, key_cols, pair_width), tile_at)
    pair_out = pl.pallas_call(
        mlp_kernel,
        name="mlp",
        compiler_params=pltpu.CompilerParams(vmem_limit_bytes=VMEM_BYTES),
        grid_spec=pltpu.PrefetchScalarGridSpec(
            num_scalar_prefetch=1,
            grid=(4,),
            in_specs=[tile_spec, tile_spec]
            + [fixed(block, key_cols, pair_width)] * 4
            + [fixed(2 * pair_width, hidden_width), fixed(1, hidden_width)]
            + [fixed(hidden_width, pair_width), fixed(1, pair_width)],
            out_specs=tile_spec,
            scratch_shapes=[pltpu.VMEM((block, key_cols, pair_width), BF16)],
        ),
        out_shape=jax.ShapeDtypeStruct(pair.shape, BF16),
        cost_estimate=pl.CostEstimate(flops=8 << 26, bytes_accessed=2 << 20, transcendentals=1 << 20),
    )(odd.astype(jnp.int32)[None], zed, pair, *landed, w_in, b_in[None], w_mlp_out, b_out[None])
    return (node_update, pair_out)


def solution(mesh):
    return jax.shard_map(
        body,
        mesh=mesh,
        in_specs=(
            P("col", None), P(), P(None, None, "row"), P(None, "col"), P("row", "col", None),
            P(), P(), P(), P(), P(), P(), P(), P(),
        ),
        out_specs=(P("row", "col"), P("row", "col", None)),
        check_vma=False,
    )
```

time: 123 us -> 132 us (1.073)
  the two profiles are of different devices: /device:TPU:1 before, /device:TPU:102 now
where the time goes in v3:
time: 132 us; the launch traced here: 131 us
  starting transfers between devices  64.1 us (49%)
  waiting for transfers between devices  36.9 us (28%)
  blocking collectives  12.8 us (10%)
  Pallas kernels  7.68 us (6%)
  local copies, waits for them, and re-layouts  5.19 us (4%)
  other arithmetic  2.87 us (2%)
    ppermute x4, starting transfers between devices, body(): lax.ppermute(jnp.transpose(tile, (1, 0, 2)), LONG, same if which == 'a' e...  33.1 us
    all_to_all x1, waiting for transfers between devices, body(): got = lax.all_to_all(sent, 'row', 0, 0, tiled=True)  18 us
    ppermute x4, waiting for transfers between devices, body(): lax.ppermute(jnp.transpose(tile, (1, 0, 2)), LONG, same if which == 'a' e...  16.9 us
    all_to_all x1, starting transfers between devices, body(): got = lax.all_to_all(sent, 'row', 0, 0, tiled=True)  14.7 us
    all_to_all x1, blocking collectives, body(): heard = lax.all_to_all(parcel, 'col', 0, 0, tiled=True)  12.8 us
    all_to_all x1, starting transfers between devices, body(): all_q = lax.all_to_all(spread, 'col', 0, 0, tiled=True)  8.17 us
    all_to_all x1, starting transfers between devices, body(): everyone = lax.all_to_all(settled, 'col', 0, 0, tiled=True)  8.1 us
    unnamed x25, local copies, waits for them, and re-layouts  3.66 us
  transfers between devices with their start and end apart: 7, of which 5 were waited for; matrix products, arithmetic and copies ran while one was open for 3% of the time, Pallas kernels for 3%

profile of v3, /device:TPU:102, one launch (start us, length us, event | category | flops | bytes accessed | tf_op | source)
XLA Modules:
  0.0 131.5 jit_solution(16155588596852806390)
XLA Ops:
  0.7 0.7 broadcast_in_dim.32.gain_ref
  1.4 0.9 copy-done.3
  2.3 0.8 copy-done.5
  3.1 1.1 shard_map.140
  4.2 8.2 %all-to-all-start = ((bf16[32,16,96]{2,1,0:T(8,128)(2,1)}), bf16[32,16,96]{2,1,0:T(8,128)(2,1)S(1)}, u32[]{:S(2)}, u32[]{:S(2)}) async-start(bf16[32,16,96]{2,1,0:T(8,128)(2,1)} %get-tuple-element.9), calls=%async_computation | async-start | bytes 262144 | tf_op jit(solution)/shard_map/all_to_all | solution.py:188
  14.1 0.9 fusion.8
  14.9 2.0 %all-to-all-done = bf16[32,16,96]{2,1,0:T(8,128)(2,1)S(1)} async-done(((bf16[32,16,96]{2,1,0:T(8,128)(2,1)}), bf16[32,16,96]{2,1,0:T(8,128)(2,1)S(1)}, u32[]{:S(2)}, u32[]{:S(2)}) %all-to-all-start) | async-done | bytes 98336 | tf_op jit(solution)/shard_map/all_to_all | solution.py:188
  17.0 0.8 pad_maximum_fusion
  17.8 14.7 %all-to-all-start.1 = ((bf16[16,16,384]{2,1,0:T(8,128)(2,1)}), bf16[16,16,384]{2,1,0:T(8,128)(2,1)S(1)}, u32[]{:S(2)}, u32[]{:S(2)}) async-start(bf16[16,16,384]{2,1,0:T(8,128)(2,1)} %pad_maximum_fusion), calls=%async_computation.1 | async-start | bytes 393216 | tf_op jit(solution)/shard_map/all_to_all | solution.py:201
  34.6 18.0 %all-to-all-done.1.got_ref = bf16[16,16,384]{2,1,0:T(8,128)(2,1)S(1)} async-done(((bf16[16,16,384]{2,1,0:T(8,128)(2,1)}), bf16[16,16,384]{2,1,0:T(8,128)(2,1)S(1)}, u32[]{:S(2)}, u32[]{:S(2)}) %all-to-all-start.1) | async-done | bytes 196640 | tf_op jit(solution)/shard_map/all_to_all | solution.py:201
  52.7 1.3 %shard_map.141 = bf16[32,16,128]{2,1,0:T(8,128)(2,1)S(1)} custom-call(bf16[16,16,384]{2,1,0:T(8,128)(2,1)S(1)} %all-to-all-done.1.got_ref, f32[64,512]{1,0:T(8,128)S(1)} %copy.35.bias_ref, f32[64,512]{1,0:T(8,128)S(1)} %copy.36.gate_ref, bf16[128,1024]{1,0:T(8,128)(2,1)S(1)} %fusion.12.select_ref), custom_call_target="tpu_custom_call" | custom-call | flops 1048576 | bytes 262144 | tf_op jit(solution)/shard_map/pallas_call | solution.py:212
  54.0 12.8 %all_to_all.20.heard_ref = bf16[32,16,128]{2,1,0:T(8,128)(2,1)S(1)} all-to-all(bf16[32,16,128]{2,1,0:T(8,128)(2,1)S(1)} %shard_map.141), channel_id=1, replica_groups=mesh['row'=16,'col'=32] {'col'}, dimensions={0} | all-to-all | bytes 262144 | tf_op jit(solution)/shard_map/all_to_all | solution.py:216
  66.8 1.0 shard_map.142
  67.8 8.1 %all-to-all-start.3 = ((bf16[32,16,128]{2,1,0:T(8,128)(2,1)}), bf16[32,16,128]{2,1,0:T(8,128)(2,1)S(1)}, u32[]{:S(2)}, u32[]{:S(2)}) async-start(bf16[32,16,128]{2,1,0:T(8,128)(2,1)} %shard_map.142), calls=%async_computation.3 | async-start | bytes 262144 | tf_op jit(solution)/shard_map/all_to_all | solution.py:218
  76.0 2.7 %collective-permute-start.3 = (bf16[16,32,128]{2,1,0:T(8,128)(2,1)S(1)}, bf16[16,32,128]{2,1,0:T(8,128)(2,1)S(1)}, u32[]{:S(2)}, u32[]{:S(2)}) collective-permute-start(bf16[16,32,128]{2,1,0:T(8,128)(2,1)S(1)} %get-tuple-element.16), channel_id=1, source_target_pairs={{0,1},{1,0},{2,33},{3,32},{4,65},{5,64},{6,97},{7,96},{8,129},{9,1... | collective-permute-start | bytes 393224 | tf_op jit(solution)/shard_map/ppermute | solution.py:196
  78.7 13.7 %collective-permute-start.2 = (bf16[16,32,128]{2,1,0:T(8,128)(2,1)S(1)}, bf16[16,32,128]{2,1,0:T(8,128)(2,1)S(1)}, u32[]{:S(2)}, u32[]{:S(2)}) collective-permute-start(bf16[16,32,128]{2,1,0:T(8,128)(2,1)S(1)} %get-tuple-element.17), channel_id=1, source_target_pairs={{0,1},{1,0},{2,33},{3,32},{4,65},{5,64},{6,97},{7,96},{8,129},{9,1... | collective-permute-start | bytes 393224 | tf_op jit(solution)/shard_map/ppermute | solution.py:196
  92.4 2.9 %collective-permute-start = (bf16[16,32,128]{2,1,0:T(8,128)(2,1)S(1)}, bf16[16,32,128]{2,1,0:T(8,128)(2,1)S(1)}, u32[]{:S(2)}, u32[]{:S(2)}) collective-permute-start(bf16[16,32,128]{2,1,0:T(8,128)(2,1)S(1)} %get-tuple-element.18), channel_id=1, source_target_pairs={{0,0},{1,1},{2,32},{3,33},{4,64},{5,65},{6,96},{7,97},{8,128},{9,1... | collective-permute-start | bytes 393224 | tf_op jit(solution)/shard_map/ppermute | solution.py:196
  95.4 13.7 %collective-permute-start.1 = (bf16[16,32,128]{2,1,0:T(8,128)(2,1)S(1)}, bf16[16,32,128]{2,1,0:T(8,128)(2,1)S(1)}, u32[]{:S(2)}, u32[]{:S(2)}) collective-permute-start(bf16[16,32,128]{2,1,0:T(8,128)(2,1)S(1)} %get-tuple-element.19), channel_id=1, source_target_pairs={{0,0},{1,1},{2,32},{3,33},{4,64},{5,65},{6,96},{7,97},{8,128},{9,1... | collective-permute-start | bytes 393224 | tf_op jit(solution)/shard_map/ppermute | solution.py:196
  109.6 7.8 %collective-permute-done.2.refs_2_ = bf16[16,32,128]{2,1,0:T(8,128)(2,1)S(1)} collective-permute-done((bf16[16,32,128]{2,1,0:T(8,128)(2,1)S(1)}, bf16[16,32,128]{2,1,0:T(8,128)(2,1)S(1)}, u32[]{:S(2)}, u32[]{:S(2)}) %collective-permute-start.2) | collective-permute-done | bytes 131104 | tf_op jit(solution)/shard_map/ppermute | solution.py:196
  117.4 5.8 %collective-permute-done.refs_0_ = bf16[16,32,128]{2,1,0:T(8,128)(2,1)S(1)} collective-permute-done((bf16[16,32,128]{2,1,0:T(8,128)(2,1)S(1)}, bf16[16,32,128]{2,1,0:T(8,128)(2,1)S(1)}, u32[]{:S(2)}, u32[]{:S(2)}) %collective-permute-start) | collective-permute-done | bytes 131104 | tf_op jit(solution)/shard_map/ppermute | solution.py:196
  123.2 3.4 %collective-permute-done.1.refs_1_ = bf16[16,32,128]{2,1,0:T(8,128)(2,1)S(1)} collective-permute-done((bf16[16,32,128]{2,1,0:T(8,128)(2,1)S(1)}, bf16[16,32,128]{2,1,0:T(8,128)(2,1)S(1)}, u32[]{:S(2)}, u32[]{:S(2)}) %collective-permute-start.1) | collective-permute-done | bytes 131104 | tf_op jit(solution)/shard_map/ppermute | solution.py:196
  126.6 0.7 copy-done.6
  127.2 3.5 %mlp.1 = bf16[64,32,128]{2,1,0:T(8,128)(2,1)} custom-call(s32[1]{0:T(128)} %bitcast.12.odd_ref, bf16[64,32,128]{2,1,0:T(8,128)(2,1)S(1)} %copy.37.zed_ref, bf16[64,32,128]{2,1,0:T(8,128)(2,1)S(1)} %copy-done.1, bf16[16,32,128]{2,1,0:T(8,128)(2,1)S(1)} %collective-permute-done.refs_0_, bf16[16,32,128]{2,1,0:T(8,128)(2,1)S(1)} %collective-permute-done.1.refs_1_, ...), custom_call_target="tpu_custom_call" | custom-call | flops 536870912 | bytes 2097152 | tf_op jit(solution)/shard_map/mlp/pallas_call | solution.py:237
  130.7 0.8 shard_map.143
  (43 shorter events, 4.3 us)
Async XLA Ops:
  0.6 31.9 %copy-start = (bf16[128,16]{0,1:T(8,128)(2,1)S(1)}, bf16[128,16]{0,1:T(8,128)(2,1)}, u32[]{:S(2)}) copy-start(bf16[128,16]{0,1:T(8,128)(2,1)} %param.19) | copy-start | bytes 12292
  0.6 11.7 %copy-start.1 = (bf16[64,32,128]{2,1,0:T(8,128)(2,1)S(1)}, bf16[64,32,128]{2,1,0:T(8,128)(2,1)}, u32[]{:S(2)}) copy-start(bf16[64,32,128]{2,1,0:T(8,128)(2,1)} %pair_ref.1) | copy-start | bytes 1572868
  1.4 0.9 copy-start.3
  2.3 0.8 copy-start.5
  4.2 12.7 %all-to-all-start = ((bf16[32,16,96]{2,1,0:T(8,128)(2,1)}), bf16[32,16,96]{2,1,0:T(8,128)(2,1)S(1)}, u32[]{:S(2)}, u32[]{:S(2)}) async-start(bf16[32,16,96]{2,1,0:T(8,128)(2,1)} %get-tuple-element.9), calls=%async_computation | async-start | bytes 262144 | tf_op jit(solution)/shard_map/all_to_all | solution.py:188
  13.4 0.7 copy-start.9
  17.8 34.9 %all-to-all-start.1 = ((bf16[16,16,384]{2,1,0:T(8,128)(2,1)}), bf16[16,16,384]{2,1,0:T(8,128)(2,1)S(1)}, u32[]{:S(2)}, u32[]{:S(2)}) async-start(bf16[16,16,384]{2,1,0:T(8,128)(2,1)} %pad_maximum_fusion), calls=%async_computation.1 | async-start | bytes 393216 | tf_op jit(solution)/shard_map/all_to_all | solution.py:201
  33.1 0.7 copy-start.10
  33.1 0.7 copy-start.11
  67.8 62.9 %all-to-all-start.3 = ((bf16[32,16,128]{2,1,0:T(8,128)(2,1)}), bf16[32,16,128]{2,1,0:T(8,128)(2,1)S(1)}, u32[]{:S(2)}, u32[]{:S(2)}) async-start(bf16[32,16,128]{2,1,0:T(8,128)(2,1)} %shard_map.142), calls=%async_computation.3 | async-start | bytes 262144 | tf_op jit(solution)/shard_map/all_to_all | solution.py:218
  76.0 33.6 %collective-permute-start.3 = (bf16[16,32,128]{2,1,0:T(8,128)(2,1)S(1)}, bf16[16,32,128]{2,1,0:T(8,128)(2,1)S(1)}, u32[]{:S(2)}, u32[]{:S(2)}) collective-permute-start(bf16[16,32,128]{2,1,0:T(8,128)(2,1)S(1)} %get-tuple-element.16), channel_id=1, source_target_pairs={{0,1},{1,0},{2,33},{3,32},{4,65},{5,64},{6,97},{7,96},{8,129},{9,1... | collective-permute-start | bytes 393224 | tf_op jit(solution)/shard_map/ppermute | solution.py:196
  78.7 38.7 %collective-permute-start.2 = (bf16[16,32,128]{2,1,0:T(8,128)(2,1)S(1)}, bf16[16,32,128]{2,1,0:T(8,128)(2,1)S(1)}, u32[]{:S(2)}, u32[]{:S(2)}) collective-permute-start(bf16[16,32,128]{2,1,0:T(8,128)(2,1)S(1)} %get-tuple-element.17), channel_id=1, source_target_pairs={{0,1},{1,0},{2,33},{3,32},{4,65},{5,64},{6,97},{7,96},{8,129},{9,1... | collective-permute-start | bytes 393224 | tf_op jit(solution)/shard_map/ppermute | solution.py:196
  92.4 30.8 %collective-permute-start = (bf16[16,32,128]{2,1,0:T(8,128)(2,1)S(1)}, bf16[16,32,128]{2,1,0:T(8,128)(2,1)S(1)}, u32[]{:S(2)}, u32[]{:S(2)}) collective-permute-start(bf16[16,32,128]{2,1,0:T(8,128)(2,1)S(1)} %get-tuple-element.18), channel_id=1, source_target_pairs={{0,0},{1,1},{2,32},{3,33},{4,64},{5,65},{6,96},{7,97},{8,128},{9,1... | collective-permute-start | bytes 393224 | tf_op jit(solution)/shard_map/ppermute | solution.py:196
  95.3 14.1 %copy-start.8 = (bf16[768,24]{0,1:T(8,128)(2,1)S(1)}, bf16[768,24]{0,1:T(8,128)(2,1)}, u32[]{:S(2)}) copy-start(bf16[768,24]{0,1:T(8,128)(2,1)} %param.16) | copy-start | bytes 110596
  95.4 31.2 %collective-permute-start.1 = (bf16[16,32,128]{2,1,0:T(8,128)(2,1)S(1)}, bf16[16,32,128]{2,1,0:T(8,128)(2,1)S(1)}, u32[]{:S(2)}, u32[]{:S(2)}) collective-permute-start(bf16[16,32,128]{2,1,0:T(8,128)(2,1)S(1)} %get-tuple-element.19), channel_id=1, source_target_pairs={{0,0},{1,1},{2,32},{3,33},{4,64},{5,65},{6,96},{7,97},{8,128},{9,1... | collective-permute-start | bytes 393224 | tf_op jit(solution)/shard_map/ppermute | solution.py:196
  109.1 17.4 %copy-start.4 = (bf16[512,128]{1,0:T(8,128)(2,1)S(1)}, bf16[512,128]{1,0:T(8,128)(2,1)}, u32[]{:S(2)}) copy-start(bf16[512,128]{1,0:T(8,128)(2,1)} %refs_6_.1) | copy-start | bytes 393220
  109.5 17.1 %copy-start.2 = (bf16[256,512]{1,0:T(8,128)(2,1)S(1)}, bf16[256,512]{1,0:T(8,128)(2,1)}, u32[]{:S(2)}) copy-start(bf16[256,512]{1,0:T(8,128)(2,1)} %refs_4_.1) | copy-start | bytes 786436
  126.5 0.7 copy-start.6
  126.5 0.7 copy-start.7

commit v4 on v3

--- a/solution.py
+++ b/solution.py
@@ -13,6 +13,7 @@
 LONG = ("row", "col")
 LANES = 128
 VMEM_BYTES = 20 << 20
+PROJECT_BYTES = 60 << 20
 
 
 def tie(value, *others):
@@ -34,11 +35,20 @@
     return values.astype(BF16).astype(F32)
 
 
-def project_kernel(nodes_ref, gain_ref, w_ref, spread_ref, own_ref):
-    normed = layer_norm(nodes_ref[...], gain_ref[...]).astype(BF16)
+def project_kernel(nodes_hbm, gain_hbm, w_hbm, spread_ref, own_ref, nodes, gain, w, sems):
+    copies = [
+        pltpu.make_async_copy(source, target, sems.at[k])
+        for k, (source, target) in enumerate(((nodes_hbm, nodes), (gain_hbm, gain), (w_hbm, w)))
+    ]
+    for copy in copies:
+        copy.start()
+    for copy in copies[:2]:
+        copy.wait()
+    normed = layer_norm(nodes[...], gain[...]).astype(BF16)
     half = normed.shape[0] // 2
+    copies[2].wait()
     for which in range(3):
-        proj = nt_dot(normed, w_ref[which])
+        proj = nt_dot(normed, w[which])
         packed = jnp.concatenate([proj[:half], proj[half:]], axis=-1).astype(BF16)
         if which == 0:
             spread_ref[...] = jnp.broadcast_to(packed[None], spread_ref.shape)
@@ -178,13 +188,23 @@
     same = [(source, base + source % 2) for source, base in ends]
     swap = [(source, base + 1 - source % 2) for source, base in ends]
 
-    spread, own = whole(
+    hbm = pl.BlockSpec(memory_space=pltpu.MemorySpace.HBM)
+    spread, own = pl.pallas_call(
         project_kernel,
-        (
+        name="project",
+        compiler_params=pltpu.CompilerParams(vmem_limit_bytes=PROJECT_BYTES),
+        in_specs=[hbm] * 3,
+        out_shape=(
             jax.ShapeDtypeStruct((cols_n, half, 2 * size), BF16),
             jax.ShapeDtypeStruct((2, half, 2 * size), BF16),
         ),
-    )(nodes, node_gain[None], jnp.transpose(w_qkv, (0, 2, 1)))
+        scratch_shapes=[
+            pltpu.VMEM(nodes.shape, BF16),
+            pltpu.VMEM(node_gain.shape, F32),
+            pltpu.VMEM((3, size, node_width), BF16),
+            pltpu.SemaphoreType.DMA((3,)),
+        ],
+    )(nodes, node_gain, jnp.transpose(w_qkv, (0, 2, 1)))
     all_q = lax.all_to_all(spread, "col", 0, 0, tiled=True)
 
     zed = layer_norm(tie(pair, own), pair_gain).astype(BF16)

time: 132 us -> 131 us (level)
  local copies, waits for them, and re-layouts: 5.19 us -> 3.4 us
    unnamed x25 -> x23, local copies, waits for them, and re-layouts: 3.66 us -> 2.61 us
where the time goes in v4:
time: 131 us; the launch traced here: 130 us
  starting transfers between devices  64.1 us (49%)
  waiting for transfers between devices  36.2 us (28%)
  blocking collectives  12.8 us (10%)
  Pallas kernels  8.57 us (7%)
  local copies, waits for them, and re-layouts  3.4 us (3%)
  other arithmetic  2.87 us (2%)
    ppermute x4, starting transfers between devices, body(): lax.ppermute(jnp.transpose(tile, (1, 0, 2)), LONG, same if which == 'a' e...  33.1 us
    all_to_all x1, waiting for transfers between devices, body(): got = lax.all_to_all(sent, 'row', 0, 0, tiled=True)  18 us
    ppermute x4, waiting for transfers between devices, body(): lax.ppermute(jnp.transpose(tile, (1, 0, 2)), LONG, same if which == 'a' e...  16.9 us
    all_to_all x1, starting transfers between devices, body(): got = lax.all_to_all(sent, 'row', 0, 0, tiled=True)  14.7 us
    all_to_all x1, blocking collectives, body(): heard = lax.all_to_all(parcel, 'col', 0, 0, tiled=True)  12.8 us
    all_to_all x1, starting transfers between devices, body(): all_q = lax.all_to_all(spread, 'col', 0, 0, tiled=True)  8.18 us
    all_to_all x1, starting transfers between devices, body(): everyone = lax.all_to_all(settled, 'col', 0, 0, tiled=True)  8.1 us
    pallas_call x1, Pallas kernels, body(): pl.pallas_call(mlp_kernel, name='mlp', compiler_params=pltpu.CompilerPara...  3.49 us
  transfers between devices with their start and end apart: 7, of which 5 were waited for; matrix products, arithmetic and copies ran while one was open for 3% of the time, Pallas kernels for 3%

profile of v4, /device:TPU:102, one launch (start us, length us, event | category | flops | bytes accessed | tf_op | source)
XLA Modules:
  0.0 129.9 jit_solution(13843912690407620180)
XLA Ops:
  0.7 2.0 %project.1 = (bf16[32,16,96]{2,1,0:T(8,128)(2,1)}, bf16[2,16,96]{2,1,0:T(8,128)(2,1)}) custom-call(bf16[32,768]{1,0:T(8,128)(2,1)} %nodes_hbm.1, f32[768]{0:T(1024)} %gain_hbm.1, bf16[3,48,768]{2,1,0:T(8,128)(2,1)} %bitcast.46), custom_call_target="tpu_custom_call" | custom-call | tf_op jit(solution)/shard_map/project/pallas_call | solution.py:192
  2.6 8.2 %all-to-all-start = ((bf16[32,16,96]{2,1,0:T(8,128)(2,1)}), bf16[32,16,96]{2,1,0:T(8,128)(2,1)S(1)}, u32[]{:S(2)}, u32[]{:S(2)}) async-start(bf16[32,16,96]{2,1,0:T(8,128)(2,1)} %get-tuple-element.9), calls=%async_computation | async-start | bytes 262144 | tf_op jit(solution)/shard_map/all_to_all | solution.py:208
  11.2 0.6 fusion.6
  11.9 0.7 copy-done.7
  12.6 0.7 copy-done.8
  13.2 0.9 fusion.8
  14.1 1.3 all-to-all-done
  15.4 0.8 pad_maximum_fusion
  16.2 14.7 %all-to-all-start.1 = ((bf16[16,16,384]{2,1,0:T(8,128)(2,1)}), bf16[16,16,384]{2,1,0:T(8,128)(2,1)S(1)}, u32[]{:S(2)}, u32[]{:S(2)}) async-start(bf16[16,16,384]{2,1,0:T(8,128)(2,1)} %pad_maximum_fusion), calls=%async_computation.1 | async-start | bytes 393216 | tf_op jit(solution)/shard_map/all_to_all | solution.py:221
  33.1 18.0 %all-to-all-done.1.got_ref = bf16[16,16,384]{2,1,0:T(8,128)(2,1)S(1)} async-done(((bf16[16,16,384]{2,1,0:T(8,128)(2,1)}), bf16[16,16,384]{2,1,0:T(8,128)(2,1)S(1)}, u32[]{:S(2)}, u32[]{:S(2)}) %all-to-all-start.1) | async-done | bytes 196640 | tf_op jit(solution)/shard_map/all_to_all | solution.py:221
  51.1 1.3 %shard_map.140 = bf16[32,16,128]{2,1,0:T(8,128)(2,1)S(1)} custom-call(bf16[16,16,384]{2,1,0:T(8,128)(2,1)S(1)} %all-to-all-done.1.got_ref, f32[64,512]{1,0:T(8,128)S(1)} %copy.35.bias_ref, f32[64,512]{1,0:T(8,128)S(1)} %copy.36.gate_ref, bf16[128,1024]{1,0:T(8,128)(2,1)S(1)} %fusion.12.select_ref), custom_call_target="tpu_custom_call" | custom-call | flops 1048576 | bytes 262144 | tf_op jit(solution)/shard_map/pallas_call | solution.py:232
  52.4 12.8 %all_to_all.20.heard_ref = bf16[32,16,128]{2,1,0:T(8,128)(2,1)S(1)} all-to-all(bf16[32,16,128]{2,1,0:T(8,128)(2,1)S(1)} %shard_map.140), channel_id=1, replica_groups=mesh['row'=16,'col'=32] {'col'}, dimensions={0} | all-to-all | bytes 262144 | tf_op jit(solution)/shard_map/all_to_all | solution.py:236
  65.2 1.0 shard_map.141
  66.3 8.1 %all-to-all-start.3 = ((bf16[32,16,128]{2,1,0:T(8,128)(2,1)}), bf16[32,16,128]{2,1,0:T(8,128)(2,1)S(1)}, u32[]{:S(2)}, u32[]{:S(2)}) async-start(bf16[32,16,128]{2,1,0:T(8,128)(2,1)} %shard_map.141), calls=%async_computation.3 | async-start | bytes 262144 | tf_op jit(solution)/shard_map/all_to_all | solution.py:238
  74.4 2.7 %collective-permute-start.3 = (bf16[16,32,128]{2,1,0:T(8,128)(2,1)S(1)}, bf16[16,32,128]{2,1,0:T(8,128)(2,1)S(1)}, u32[]{:S(2)}, u32[]{:S(2)}) collective-permute-start(bf16[16,32,128]{2,1,0:T(8,128)(2,1)S(1)} %get-tuple-element.16), channel_id=1, source_target_pairs={{0,1},{1,0},{2,33},{3,32},{4,65},{5,64},{6,97},{7,96},{8,129},{9,1... | collective-permute-start | bytes 393224 | tf_op jit(solution)/shard_map/ppermute | solution.py:216
  77.2 13.7 %collective-permute-start.2 = (bf16[16,32,128]{2,1,0:T(8,128)(2,1)S(1)}, bf16[16,32,128]{2,1,0:T(8,128)(2,1)S(1)}, u32[]{:S(2)}, u32[]{:S(2)}) collective-permute-start(bf16[16,32,128]{2,1,0:T(8,128)(2,1)S(1)} %get-tuple-element.17), channel_id=1, source_target_pairs={{0,1},{1,0},{2,33},{3,32},{4,65},{5,64},{6,97},{7,96},{8,129},{9,1... | collective-permute-start | bytes 393224 | tf_op jit(solution)/shard_map/ppermute | solution.py:216
  90.8 2.9 %collective-permute-start = (bf16[16,32,128]{2,1,0:T(8,128)(2,1)S(1)}, bf16[16,32,128]{2,1,0:T(8,128)(2,1)S(1)}, u32[]{:S(2)}, u32[]{:S(2)}) collective-permute-start(bf16[16,32,128]{2,1,0:T(8,128)(2,1)S(1)} %get-tuple-element.18), channel_id=1, source_target_pairs={{0,0},{1,1},{2,32},{3,33},{4,64},{5,65},{6,96},{7,97},{8,128},{9,1... | collective-permute-start | bytes 393224 | tf_op jit(solution)/shard_map/ppermute | solution.py:216
  93.8 13.7 %collective-permute-start.1 = (bf16[16,32,128]{2,1,0:T(8,128)(2,1)S(1)}, bf16[16,32,128]{2,1,0:T(8,128)(2,1)S(1)}, u32[]{:S(2)}, u32[]{:S(2)}) collective-permute-start(bf16[16,32,128]{2,1,0:T(8,128)(2,1)S(1)} %get-tuple-element.19), channel_id=1, source_target_pairs={{0,0},{1,1},{2,32},{3,33},{4,64},{5,65},{6,96},{7,97},{8,128},{9,1... | collective-permute-start | bytes 393224 | tf_op jit(solution)/shard_map/ppermute | solution.py:216
  108.1 7.7 %collective-permute-done.2.refs_2_ = bf16[16,32,128]{2,1,0:T(8,128)(2,1)S(1)} collective-permute-done((bf16[16,32,128]{2,1,0:T(8,128)(2,1)S(1)}, bf16[16,32,128]{2,1,0:T(8,128)(2,1)S(1)}, u32[]{:S(2)}, u32[]{:S(2)}) %collective-permute-start.2) | collective-permute-done | bytes 131104 | tf_op jit(solution)/shard_map/ppermute | solution.py:216
  115.8 5.8 %collective-permute-done.refs_0_ = bf16[16,32,128]{2,1,0:T(8,128)(2,1)S(1)} collective-permute-done((bf16[16,32,128]{2,1,0:T(8,128)(2,1)S(1)}, bf16[16,32,128]{2,1,0:T(8,128)(2,1)S(1)}, u32[]{:S(2)}, u32[]{:S(2)}) %collective-permute-start) | collective-permute-done | bytes 131104 | tf_op jit(solution)/shard_map/ppermute | solution.py:216
  121.6 3.4 %collective-permute-done.1.refs_1_ = bf16[16,32,128]{2,1,0:T(8,128)(2,1)S(1)} collective-permute-done((bf16[16,32,128]{2,1,0:T(8,128)(2,1)S(1)}, bf16[16,32,128]{2,1,0:T(8,128)(2,1)S(1)}, u32[]{:S(2)}, u32[]{:S(2)}) %collective-permute-start.1) | collective-permute-done | bytes 131104 | tf_op jit(solution)/shard_map/ppermute | solution.py:216
  125.0 0.7 copy-done.4
  125.7 3.5 %mlp.1 = bf16[64,32,128]{2,1,0:T(8,128)(2,1)} custom-call(s32[1]{0:T(128)} %bitcast.12.odd_ref, bf16[64,32,128]{2,1,0:T(8,128)(2,1)S(1)} %copy.37.zed_ref, bf16[64,32,128]{2,1,0:T(8,128)(2,1)S(1)} %copy-done.1, bf16[16,32,128]{2,1,0:T(8,128)(2,1)S(1)} %collective-permute-done.refs_0_, bf16[16,32,128]{2,1,0:T(8,128)(2,1)S(1)} %collective-permute-done.1.refs_1_, ...), custom_call_target="tpu_custom_call" | custom-call | flops 536870912 | bytes 2097152 | tf_op jit(solution)/shard_map/mlp/pallas_call | solution.py:257
  129.2 0.8 shard_map.142
  (40 shorter events, 3.0 us)
Async XLA Ops:
  0.6 30.4 %copy-start = (bf16[128,16]{0,1:T(8,128)(2,1)S(1)}, bf16[128,16]{0,1:T(8,128)(2,1)}, u32[]{:S(2)}) copy-start(bf16[128,16]{0,1:T(8,128)(2,1)} %param.19) | copy-start | bytes 12292
  0.6 10.2 %copy-start.1 = (bf16[64,32,128]{2,1,0:T(8,128)(2,1)S(1)}, bf16[64,32,128]{2,1,0:T(8,128)(2,1)}, u32[]{:S(2)}) copy-start(bf16[64,32,128]{2,1,0:T(8,128)(2,1)} %pair_ref.1) | copy-start | bytes 1572868
  2.6 12.7 %all-to-all-start = ((bf16[32,16,96]{2,1,0:T(8,128)(2,1)}), bf16[32,16,96]{2,1,0:T(8,128)(2,1)S(1)}, u32[]{:S(2)}, u32[]{:S(2)}) async-start(bf16[32,16,96]{2,1,0:T(8,128)(2,1)} %get-tuple-element.9), calls=%async_computation | async-start | bytes 262144 | tf_op jit(solution)/shard_map/all_to_all | solution.py:208
  11.9 0.7 copy-start.7
  12.6 0.7 copy-start.8
  16.2 34.9 %all-to-all-start.1 = ((bf16[16,16,384]{2,1,0:T(8,128)(2,1)}), bf16[16,16,384]{2,1,0:T(8,128)(2,1)S(1)}, u32[]{:S(2)}, u32[]{:S(2)}) async-start(bf16[16,16,384]{2,1,0:T(8,128)(2,1)} %pad_maximum_fusion), calls=%async_computation.1 | async-start | bytes 393216 | tf_op jit(solution)/shard_map/all_to_all | solution.py:221
  31.5 0.7 copy-start.9
  31.5 0.7 copy-start.10
  66.3 62.9 %all-to-all-start.3 = ((bf16[32,16,128]{2,1,0:T(8,128)(2,1)}), bf16[32,16,128]{2,1,0:T(8,128)(2,1)S(1)}, u32[]{:S(2)}, u32[]{:S(2)}) async-start(bf16[32,16,128]{2,1,0:T(8,128)(2,1)} %shard_map.141), calls=%async_computation.3 | async-start | bytes 262144 | tf_op jit(solution)/shard_map/all_to_all | solution.py:238
  74.4 33.6 %collective-permute-start.3 = (bf16[16,32,128]{2,1,0:T(8,128)(2,1)S(1)}, bf16[16,32,128]{2,1,0:T(8,128)(2,1)S(1)}, u32[]{:S(2)}, u32[]{:S(2)}) collective-permute-start(bf16[16,32,128]{2,1,0:T(8,128)(2,1)S(1)} %get-tuple-element.16), channel_id=1, source_target_pairs={{0,1},{1,0},{2,33},{3,32},{4,65},{5,64},{6,97},{7,96},{8,129},{9,1... | collective-permute-start | bytes 393224 | tf_op jit(solution)/shard_map/ppermute | solution.py:216
  77.2 38.7 %collective-permute-start.2 = (bf16[16,32,128]{2,1,0:T(8,128)(2,1)S(1)}, bf16[16,32,128]{2,1,0:T(8,128)(2,1)S(1)}, u32[]{:S(2)}, u32[]{:S(2)}) collective-permute-start(bf16[16,32,128]{2,1,0:T(8,128)(2,1)S(1)} %get-tuple-element.17), channel_id=1, source_target_pairs={{0,1},{1,0},{2,33},{3,32},{4,65},{5,64},{6,97},{7,96},{8,129},{9,1... | collective-permute-start | bytes 393224 | tf_op jit(solution)/shard_map/ppermute | solution.py:216
  90.8 30.8 %collective-permute-start = (bf16[16,32,128]{2,1,0:T(8,128)(2,1)S(1)}, bf16[16,32,128]{2,1,0:T(8,128)(2,1)S(1)}, u32[]{:S(2)}, u32[]{:S(2)}) collective-permute-start(bf16[16,32,128]{2,1,0:T(8,128)(2,1)S(1)} %get-tuple-element.18), channel_id=1, source_target_pairs={{0,0},{1,1},{2,32},{3,33},{4,64},{5,65},{6,96},{7,97},{8,128},{9,1... | collective-permute-start | bytes 393224 | tf_op jit(solution)/shard_map/ppermute | solution.py:216
  93.8 14.1 %copy-start.6 = (bf16[768,24]{0,1:T(8,128)(2,1)S(1)}, bf16[768,24]{0,1:T(8,128)(2,1)}, u32[]{:S(2)}) copy-start(bf16[768,24]{0,1:T(8,128)(2,1)} %param.16) | copy-start | bytes 110596
  93.8 31.2 %collective-permute-start.1 = (bf16[16,32,128]{2,1,0:T(8,128)(2,1)S(1)}, bf16[16,32,128]{2,1,0:T(8,128)(2,1)S(1)}, u32[]{:S(2)}, u32[]{:S(2)}) collective-permute-start(bf16[16,32,128]{2,1,0:T(8,128)(2,1)S(1)} %get-tuple-element.19), channel_id=1, source_target_pairs={{0,0},{1,1},{2,32},{3,33},{4,64},{5,65},{6,96},{7,97},{8,128},{9,1... | collective-permute-start | bytes 393224 | tf_op jit(solution)/shard_map/ppermute | solution.py:216
  107.5 17.5 %copy-start.3 = (bf16[512,128]{1,0:T(8,128)(2,1)S(1)}, bf16[512,128]{1,0:T(8,128)(2,1)}, u32[]{:S(2)}) copy-start(bf16[512,128]{1,0:T(8,128)(2,1)} %refs_6_.1) | copy-start | bytes 393220
  107.9 17.1 %copy-start.2 = (bf16[256,512]{1,0:T(8,128)(2,1)S(1)}, bf16[256,512]{1,0:T(8,128)(2,1)}, u32[]{:S(2)}) copy-start(bf16[256,512]{1,0:T(8,128)(2,1)} %refs_4_.1) | copy-start | bytes 786436
  125.0 0.7 copy-start.4
  125.0 0.7 copy-start.5

commit v5 on v4

--- a/solution.py
+++ b/solution.py
@@ -56,6 +56,13 @@
             own_ref[which - 1] = packed
 
 
+def pack_kernel(all_ref, own_ref, out_ref):
+    own = jnp.concatenate([own_ref[0].astype(F32), own_ref[1].astype(F32)], axis=-1)
+    for r in range(out_ref.shape[0]):
+        left, right = all_ref[2 * r].astype(F32), all_ref[2 * r + 1].astype(F32)
+        out_ref[r] = jnp.concatenate([left, right, own], axis=-1).astype(BF16)
+
+
 def attend_kernel(got_ref, bias_ref, gate_ref, select_ref, parcel_ref, *, heads, size):
     half = got_ref.shape[1]
     pairs = heads // 2
@@ -215,9 +222,7 @@
         tile = lax.dynamic_slice_in_dim(zed, mine * key_cols, key_cols, 0)[:, part * rows : (part + 1) * rows]
         landed.append(lax.ppermute(jnp.transpose(tile, (1, 0, 2)), LONG, same if which == "a" else swap))
 
-    blocks = all_q.reshape(rows_n, 2, half, 2 * size)
-    mine = [jnp.broadcast_to(own[k][None], (rows_n, half, 2 * size)) for k in range(2)]
-    sent = jnp.concatenate([blocks[:, 0], blocks[:, 1]] + mine, axis=-1)
+    sent = whole(pack_kernel, jax.ShapeDtypeStruct((rows_n, half, 8 * size), BF16))(all_q, own)
     got = lax.all_to_all(sent, "row", 0, 0, tiled=True)
 
     pair_bias = jnp.einsum("ijc,ch->ijh", pair, w_bias, preferred_element_type=F32)

time: 131 us -> 130 us (level)
  no operation moved by 1% of the time
where the time goes in v5:
time: 130 us
  starting transfers between devices  64.1 us (49%)
  waiting for transfers between devices  36.9 us (28%)
  blocking collectives  12.8 us (10%)
  Pallas kernels  9.41 us (7%)
  local copies, waits for them, and re-layouts  2.68 us (2%)
  other arithmetic  2.03 us (2%)
    ppermute x4, starting transfers between devices, body(): lax.ppermute(jnp.transpose(tile, (1, 0, 2)), LONG, same if which == 'a' e...  33.1 us
    all_to_all x1, waiting for transfers between devices, body(): got = lax.all_to_all(sent, 'row', 0, 0, tiled=True)  18 us
    ppermute x4, waiting for transfers between devices, body(): lax.ppermute(jnp.transpose(tile, (1, 0, 2)), LONG, same if which == 'a' e...  16.9 us
    all_to_all x1, starting transfers between devices, body(): got = lax.all_to_all(sent, 'row', 0, 0, tiled=True)  14.7 us
    all_to_all x1, blocking collectives, body(): heard = lax.all_to_all(parcel, 'col', 0, 0, tiled=True)  12.8 us
    all_to_all x1, starting transfers between devices, body(): all_q = lax.all_to_all(spread, 'col', 0, 0, tiled=True)  8.18 us
    all_to_all x1, starting transfers between devices, body(): everyone = lax.all_to_all(settled, 'col', 0, 0, tiled=True)  8.11 us
    pallas_call x1, Pallas kernels, body(): pl.pallas_call(mlp_kernel, name='mlp', compiler_params=pltpu.CompilerPara...  3.49 us
  transfers between devices with their start and end apart: 7, of which 5 were waited for; matrix products, arithmetic and copies ran while one was open for 3% of the time, Pallas kernels for 3%

profile of v5, /device:TPU:102, one launch (start us, length us, event | category | flops | bytes accessed | tf_op | source)
XLA Modules:
  0.0 129.9 jit_solution(14284372121877817173)
XLA Ops:
  0.7 2.0 %project.1 = (bf16[32,16,96]{2,1,0:T(8,128)(2,1)}, bf16[2,16,96]{2,1,0:T(8,128)(2,1)}) custom-call(bf16[32,768]{1,0:T(8,128)(2,1)} %nodes_hbm.1, f32[768]{0:T(1024)} %gain_hbm.1, bf16[3,48,768]{2,1,0:T(8,128)(2,1)} %bitcast.32), custom_call_target="tpu_custom_call" | custom-call | tf_op jit(solution)/shard_map/project/pallas_call | solution.py:199
  2.6 8.2 %all-to-all-start = ((bf16[32,16,96]{2,1,0:T(8,128)(2,1)}), bf16[32,16,96]{2,1,0:T(8,128)(2,1)S(1)}, u32[]{:S(2)}, u32[]{:S(2)}) async-start(bf16[32,16,96]{2,1,0:T(8,128)(2,1)} %get-tuple-element.9), calls=%async_computation | async-start | bytes 262144 | tf_op jit(solution)/shard_map/all_to_all | solution.py:215
  11.2 0.6 fusion.6
  11.9 0.6 copy-done.8
  12.5 0.9 fusion.8
  13.4 2.0 %all-to-all-done.all_ref = bf16[32,16,96]{2,1,0:T(8,128)(2,1)S(1)} async-done(((bf16[32,16,96]{2,1,0:T(8,128)(2,1)}), bf16[32,16,96]{2,1,0:T(8,128)(2,1)S(1)}, u32[]{:S(2)}, u32[]{:S(2)}) %all-to-all-start) | async-done | bytes 98336 | tf_op jit(solution)/shard_map/all_to_all | solution.py:215
  15.4 0.8 shard_map.140
  16.2 14.7 %all-to-all-start.1 = ((bf16[16,16,384]{2,1,0:T(8,128)(2,1)}), bf16[16,16,384]{2,1,0:T(8,128)(2,1)S(1)}, u32[]{:S(2)}, u32[]{:S(2)}) async-start(bf16[16,16,384]{2,1,0:T(8,128)(2,1)} %shard_map.140), calls=%async_computation.1 | async-start | bytes 393216 | tf_op jit(solution)/shard_map/all_to_all | solution.py:226
  31.6 0.6 copy-done.9
  33.0 18.0 %all-to-all-done.1.got_ref = bf16[16,16,384]{2,1,0:T(8,128)(2,1)S(1)} async-done(((bf16[16,16,384]{2,1,0:T(8,128)(2,1)}), bf16[16,16,384]{2,1,0:T(8,128)(2,1)S(1)}, u32[]{:S(2)}, u32[]{:S(2)}) %all-to-all-start.1) | async-done | bytes 196640 | tf_op jit(solution)/shard_map/all_to_all | solution.py:226
  51.0 1.3 %shard_map.141 = bf16[32,16,128]{2,1,0:T(8,128)(2,1)S(1)} custom-call(bf16[16,16,384]{2,1,0:T(8,128)(2,1)S(1)} %all-to-all-done.1.got_ref, f32[64,512]{1,0:T(8,128)S(1)} %copy.31.bias_ref, f32[64,512]{1,0:T(8,128)S(1)} %copy.32.gate_ref, bf16[128,1024]{1,0:T(8,128)(2,1)S(1)} %fusion.12.select_ref), custom_call_target="tpu_custom_call" | custom-call | flops 1048576 | bytes 262144 | tf_op jit(solution)/shard_map/pallas_call | solution.py:237
  52.4 12.8 %all_to_all.20.heard_ref = bf16[32,16,128]{2,1,0:T(8,128)(2,1)S(1)} all-to-all(bf16[32,16,128]{2,1,0:T(8,128)(2,1)S(1)} %shard_map.141), channel_id=1, replica_groups=mesh['row'=16,'col'=32] {'col'}, dimensions={0} | all-to-all | bytes 262144 | tf_op jit(solution)/shard_map/all_to_all | solution.py:241
  65.2 1.0 shard_map.142
  66.2 8.1 %all-to-all-start.3 = ((bf16[32,16,128]{2,1,0:T(8,128)(2,1)}), bf16[32,16,128]{2,1,0:T(8,128)(2,1)S(1)}, u32[]{:S(2)}, u32[]{:S(2)}) async-start(bf16[32,16,128]{2,1,0:T(8,128)(2,1)} %shard_map.142), calls=%async_computation.3 | async-start | bytes 262144 | tf_op jit(solution)/shard_map/all_to_all | solution.py:243
  74.4 2.7 %collective-permute-start.3 = (bf16[16,32,128]{2,1,0:T(8,128)(2,1)S(1)}, bf16[16,32,128]{2,1,0:T(8,128)(2,1)S(1)}, u32[]{:S(2)}, u32[]{:S(2)}) collective-permute-start(bf16[16,32,128]{2,1,0:T(8,128)(2,1)S(1)} %get-tuple-element.16), channel_id=1, source_target_pairs={{0,1},{1,0},{2,33},{3,32},{4,65},{5,64},{6,97},{7,96},{8,129},{9,1... | collective-permute-start | bytes 393224 | tf_op jit(solution)/shard_map/ppermute | solution.py:223
  77.1 13.7 %collective-permute-start.2 = (bf16[16,32,128]{2,1,0:T(8,128)(2,1)S(1)}, bf16[16,32,128]{2,1,0:T(8,128)(2,1)S(1)}, u32[]{:S(2)}, u32[]{:S(2)}) collective-permute-start(bf16[16,32,128]{2,1,0:T(8,128)(2,1)S(1)} %get-tuple-element.17), channel_id=1, source_target_pairs={{0,1},{1,0},{2,33},{3,32},{4,65},{5,64},{6,97},{7,96},{8,129},{9,1... | collective-permute-start | bytes 393224 | tf_op jit(solution)/shard_map/ppermute | solution.py:223
  90.8 2.9 %collective-permute-start = (bf16[16,32,128]{2,1,0:T(8,128)(2,1)S(1)}, bf16[16,32,128]{2,1,0:T(8,128)(2,1)S(1)}, u32[]{:S(2)}, u32[]{:S(2)}) collective-permute-start(bf16[16,32,128]{2,1,0:T(8,128)(2,1)S(1)} %get-tuple-element.18), channel_id=1, source_target_pairs={{0,0},{1,1},{2,32},{3,33},{4,64},{5,65},{6,96},{7,97},{8,128},{9,1... | collective-permute-start | bytes 393224 | tf_op jit(solution)/shard_map/ppermute | solution.py:223
  93.8 13.7 %collective-permute-start.1 = (bf16[16,32,128]{2,1,0:T(8,128)(2,1)S(1)}, bf16[16,32,128]{2,1,0:T(8,128)(2,1)S(1)}, u32[]{:S(2)}, u32[]{:S(2)}) collective-permute-start(bf16[16,32,128]{2,1,0:T(8,128)(2,1)S(1)} %get-tuple-element.19), channel_id=1, source_target_pairs={{0,0},{1,1},{2,32},{3,33},{4,64},{5,65},{6,96},{7,97},{8,128},{9,1... | collective-permute-start | bytes 393224 | tf_op jit(solution)/shard_map/ppermute | solution.py:223
  108.1 7.7 %collective-permute-done.2.refs_2_ = bf16[16,32,128]{2,1,0:T(8,128)(2,1)S(1)} collective-permute-done((bf16[16,32,128]{2,1,0:T(8,128)(2,1)S(1)}, bf16[16,32,128]{2,1,0:T(8,128)(2,1)S(1)}, u32[]{:S(2)}, u32[]{:S(2)}) %collective-permute-start.2) | collective-permute-done | bytes 131104 | tf_op jit(solution)/shard_map/ppermute | solution.py:223
  115.8 5.8 %collective-permute-done.refs_0_ = bf16[16,32,128]{2,1,0:T(8,128)(2,1)S(1)} collective-permute-done((bf16[16,32,128]{2,1,0:T(8,128)(2,1)S(1)}, bf16[16,32,128]{2,1,0:T(8,128)(2,1)S(1)}, u32[]{:S(2)}, u32[]{:S(2)}) %collective-permute-start) | collective-permute-done | bytes 131104 | tf_op jit(solution)/shard_map/ppermute | solution.py:223
  121.6 3.4 %collective-permute-done.1.refs_1_ = bf16[16,32,128]{2,1,0:T(8,128)(2,1)S(1)} collective-permute-done((bf16[16,32,128]{2,1,0:T(8,128)(2,1)S(1)}, bf16[16,32,128]{2,1,0:T(8,128)(2,1)S(1)}, u32[]{:S(2)}, u32[]{:S(2)}) %collective-permute-start.1) | collective-permute-done | bytes 131104 | tf_op jit(solution)/shard_map/ppermute | solution.py:223
  125.0 0.7 copy-done.5
  125.6 3.5 %mlp.1 = bf16[64,32,128]{2,1,0:T(8,128)(2,1)} custom-call(s32[1]{0:T(128)} %bitcast.7.odd_ref, bf16[64,32,128]{2,1,0:T(8,128)(2,1)S(1)} %copy.33.zed_ref, bf16[64,32,128]{2,1,0:T(8,128)(2,1)S(1)} %copy-done.1, bf16[16,32,128]{2,1,0:T(8,128)(2,1)S(1)} %collective-permute-done.refs_0_, bf16[16,32,128]{2,1,0:T(8,128)(2,1)S(1)} %collective-permute-done.1.refs_1_, ...), custom_call_target="tpu_custom_call" | custom-call | flops 536870912 | bytes 2097152 | tf_op jit(solution)/shard_map/mlp/pallas_call | solution.py:262
  129.1 0.8 shard_map.143
  (36 shorter events, 2.4 us)
Async XLA Ops:
  0.6 30.3 %copy-start = (bf16[128,16]{0,1:T(8,128)(2,1)S(1)}, bf16[128,16]{0,1:T(8,128)(2,1)}, u32[]{:S(2)}) copy-start(bf16[128,16]{0,1:T(8,128)(2,1)} %param.19) | copy-start | bytes 12292
  0.6 10.2 %copy-start.1 = (bf16[64,32,128]{2,1,0:T(8,128)(2,1)S(1)}, bf16[64,32,128]{2,1,0:T(8,128)(2,1)}, u32[]{:S(2)}) copy-start(bf16[64,32,128]{2,1,0:T(8,128)(2,1)} %pair_ref.1) | copy-start | bytes 1572868
  2.6 12.7 %all-to-all-start = ((bf16[32,16,96]{2,1,0:T(8,128)(2,1)}), bf16[32,16,96]{2,1,0:T(8,128)(2,1)S(1)}, u32[]{:S(2)}, u32[]{:S(2)}) async-start(bf16[32,16,96]{2,1,0:T(8,128)(2,1)} %get-tuple-element.9), calls=%async_computation | async-start | bytes 262144 | tf_op jit(solution)/shard_map/all_to_all | solution.py:215
  11.9 0.7 copy-start.8
  12.5 2.8 %copy-start.4 = (bf16[2,16,96]{2,1,0:T(8,128)(2,1)S(1)}, bf16[2,16,96]{2,1,0:T(8,128)(2,1)}, u32[]{:S(2)}) copy-start(bf16[2,16,96]{2,1,0:T(8,128)(2,1)} %get-tuple-element.10.own_ref) | copy-start | bytes 18436
  16.2 34.9 %all-to-all-start.1 = ((bf16[16,16,384]{2,1,0:T(8,128)(2,1)}), bf16[16,16,384]{2,1,0:T(8,128)(2,1)S(1)}, u32[]{:S(2)}, u32[]{:S(2)}) async-start(bf16[16,16,384]{2,1,0:T(8,128)(2,1)} %shard_map.140), calls=%async_computation.1 | async-start | bytes 393216 | tf_op jit(solution)/shard_map/all_to_all | solution.py:226
  31.5 0.7 copy-start.9
  31.5 0.7 copy-start.10
  66.2 62.9 %all-to-all-start.3 = ((bf16[32,16,128]{2,1,0:T(8,128)(2,1)}), bf16[32,16,128]{2,1,0:T(8,128)(2,1)S(1)}, u32[]{:S(2)}, u32[]{:S(2)}) async-start(bf16[32,16,128]{2,1,0:T(8,128)(2,1)} %shard_map.142), calls=%async_computation.3 | async-start | bytes 262144 | tf_op jit(solution)/shard_map/all_to_all | solution.py:243
  74.4 33.6 %collective-permute-start.3 = (bf16[16,32,128]{2,1,0:T(8,128)(2,1)S(1)}, bf16[16,32,128]{2,1,0:T(8,128)(2,1)S(1)}, u32[]{:S(2)}, u32[]{:S(2)}) collective-permute-start(bf16[16,32,128]{2,1,0:T(8,128)(2,1)S(1)} %get-tuple-element.16), channel_id=1, source_target_pairs={{0,1},{1,0},{2,33},{3,32},{4,65},{5,64},{6,97},{7,96},{8,129},{9,1... | collective-permute-start | bytes 393224 | tf_op jit(solution)/shard_map/ppermute | solution.py:223
  77.1 38.7 %collective-permute-start.2 = (bf16[16,32,128]{2,1,0:T(8,128)(2,1)S(1)}, bf16[16,32,128]{2,1,0:T(8,128)(2,1)S(1)}, u32[]{:S(2)}, u32[]{:S(2)}) collective-permute-start(bf16[16,32,128]{2,1,0:T(8,128)(2,1)S(1)} %get-tuple-element.17), channel_id=1, source_target_pairs={{0,1},{1,0},{2,33},{3,32},{4,65},{5,64},{6,97},{7,96},{8,129},{9,1... | collective-permute-start | bytes 393224 | tf_op jit(solution)/shard_map/ppermute | solution.py:223
  90.8 30.8 %collective-permute-start = (bf16[16,32,128]{2,1,0:T(8,128)(2,1)S(1)}, bf16[16,32,128]{2,1,0:T(8,128)(2,1)S(1)}, u32[]{:S(2)}, u32[]{:S(2)}) collective-permute-start(bf16[16,32,128]{2,1,0:T(8,128)(2,1)S(1)} %get-tuple-element.18), channel_id=1, source_target_pairs={{0,0},{1,1},{2,32},{3,33},{4,64},{5,65},{6,96},{7,97},{8,128},{9,1... | collective-permute-start | bytes 393224 | tf_op jit(solution)/shard_map/ppermute | solution.py:223
  93.7 14.1 %copy-start.7 = (bf16[768,24]{0,1:T(8,128)(2,1)S(1)}, bf16[768,24]{0,1:T(8,128)(2,1)}, u32[]{:S(2)}) copy-start(bf16[768,24]{0,1:T(8,128)(2,1)} %param.16) | copy-start | bytes 110596
  93.8 31.2 %collective-permute-start.1 = (bf16[16,32,128]{2,1,0:T(8,128)(2,1)S(1)}, bf16[16,32,128]{2,1,0:T(8,128)(2,1)S(1)}, u32[]{:S(2)}, u32[]{:S(2)}) collective-permute-start(bf16[16,32,128]{2,1,0:T(8,128)(2,1)S(1)} %get-tuple-element.19), channel_id=1, source_target_pairs={{0,0},{1,1},{2,32},{3,33},{4,64},{5,65},{6,96},{7,97},{8,128},{9,1... | collective-permute-start | bytes 393224 | tf_op jit(solution)/shard_map/ppermute | solution.py:223
  107.5 17.5 %copy-start.3 = (bf16[512,128]{1,0:T(8,128)(2,1)S(1)}, bf16[512,128]{1,0:T(8,128)(2,1)}, u32[]{:S(2)}) copy-start(bf16[512,128]{1,0:T(8,128)(2,1)} %refs_6_.1) | copy-start | bytes 393220
  107.9 17.1 %copy-start.2 = (bf16[256,512]{1,0:T(8,128)(2,1)S(1)}, bf16[256,512]{1,0:T(8,128)(2,1)}, u32[]{:S(2)}) copy-start(bf16[256,512]{1,0:T(8,128)(2,1)} %refs_4_.1) | copy-start | bytes 786436
  124.9 0.7 copy-start.5
  125.0 0.7 copy-start.6

commit v6 on v5

--- a/solution.py
+++ b/solution.py
@@ -214,12 +214,16 @@
     )(nodes, node_gain, jnp.transpose(w_qkv, (0, 2, 1)))
     all_q = lax.all_to_all(spread, "col", 0, 0, tiled=True)
 
-    zed = layer_norm(tie(pair, own), pair_gain).astype(BF16)
     landed = []
-    for which, part in PIECES:
+    for index, (which, part) in enumerate(PIECES):
         mine = odd if which == "a" else 1 - odd
         rows = key_cols // 2
-        tile = lax.dynamic_slice_in_dim(zed, mine * key_cols, key_cols, 0)[:, part * rows : (part + 1) * rows]
+        if index:
+            tile = lax.dynamic_slice_in_dim(zed, mine * key_cols, key_cols, 0)[:, part * rows : (part + 1) * rows]
+        else:
+            raw = lax.dynamic_slice_in_dim(pair, mine * key_cols, key_cols, 0)[:, part * rows : (part + 1) * rows]
+            tile = layer_norm(tie(raw, own), pair_gain).astype(BF16)
+            zed = layer_norm(tie(pair, tile), pair_gain).astype(BF16)
         landed.append(lax.ppermute(jnp.transpose(tile, (1, 0, 2)), LONG, same if which == "a" else swap))
 
     sent = whole(pack_kernel, jax.ShapeDtypeStruct((rows_n, half, 8 * size), BF16))(all_q, own)

time: 130 us -> 130 us (level)
  waiting for transfers between devices: 36.9 us -> 35.4 us
  transfers between devices with their start and end apart: 7 -> 7, of which waited for: 5 -> 5; matrix products, arithmetic and copies ran while one was open for 3% -> 4% of each run, Pallas kernels for 3% -> 3%
where the time goes in v6:
time: 130 us; the launch traced here: 129 us
  starting transfers between devices  64.1 us (49%)
  waiting for transfers between devices  35.4 us (27%)
  blocking collectives  12.8 us (10%)
  Pallas kernels  9.39 us (7%)
  local copies, waits for them, and re-layouts  2.89 us (2%)
  other arithmetic  2.64 us (2%)
    ppermute x4, starting transfers between devices, body(): lax.ppermute(jnp.transpose(tile, (1, 0, 2)), LONG, same if which == 'a' e...  33.1 us
    all_to_all x1, waiting for transfers between devices, body(): got = lax.all_to_all(sent, 'row', 0, 0, tiled=True)  18 us
    ppermute x4, waiting for transfers between devices, body(): lax.ppermute(jnp.transpose(tile, (1, 0, 2)), LONG, same if which == 'a' e...  16.1 us
    all_to_all x1, starting transfers between devices, body(): got = lax.all_to_all(sent, 'row', 0, 0, tiled=True)  14.7 us
    all_to_all x1, blocking collectives, body(): heard = lax.all_to_all(parcel, 'col', 0, 0, tiled=True)  12.8 us
    all_to_all x1, starting transfers between devices, body(): all_q = lax.all_to_all(spread, 'col', 0, 0, tiled=True)  8.18 us
    all_to_all x1, starting transfers between devices, body(): everyone = lax.all_to_all(settled, 'col', 0, 0, tiled=True)  8.1 us
    pallas_call x1, Pallas kernels, body(): pl.pallas_call(mlp_kernel, name='mlp', compiler_params=pltpu.CompilerPara...  3.49 us
  transfers between devices with their start and end apart: 7, of which 5 were waited for; matrix products, arithmetic and copies ran while one was open for 4% of the time, Pallas kernels for 3%

profile of v6, /device:TPU:102, one launch (start us, length us, event | category | flops | bytes accessed | tf_op | source)
XLA Modules:
  0.0 129.3 jit_solution(12788884060400920562)
XLA Ops:
  0.7 2.0 %project.1 = (bf16[32,16,96]{2,1,0:T(8,128)(2,1)}, bf16[2,16,96]{2,1,0:T(8,128)(2,1)}) custom-call(bf16[32,768]{1,0:T(8,128)(2,1)} %nodes_hbm.1, f32[768]{0:T(1024)} %gain_hbm.1, bf16[3,48,768]{2,1,0:T(8,128)(2,1)} %bitcast.32), custom_call_target="tpu_custom_call" | custom-call | tf_op jit(solution)/shard_map/project/pallas_call | solution.py:199
  2.6 8.2 %all-to-all-start = ((bf16[32,16,96]{2,1,0:T(8,128)(2,1)}), bf16[32,16,96]{2,1,0:T(8,128)(2,1)S(1)}, u32[]{:S(2)}, u32[]{:S(2)}) async-start(bf16[32,16,96]{2,1,0:T(8,128)(2,1)} %get-tuple-element.10), calls=%async_computation | async-start | bytes 262144 | tf_op jit(solution)/shard_map/all_to_all | solution.py:215
  11.9 0.6 fusion.6
  12.6 0.6 copy-done.8
  13.2 0.9 fusion.8
  14.1 1.3 all-to-all-done.all_ref
  15.4 0.8 shard_map.140
  16.2 14.7 %all-to-all-start.1 = ((bf16[16,16,384]{2,1,0:T(8,128)(2,1)}), bf16[16,16,384]{2,1,0:T(8,128)(2,1)S(1)}, u32[]{:S(2)}, u32[]{:S(2)}) async-start(bf16[16,16,384]{2,1,0:T(8,128)(2,1)} %shard_map.140), calls=%async_computation.1 | async-start | bytes 393216 | tf_op jit(solution)/shard_map/all_to_all | solution.py:230
  31.6 0.6 copy-done.9
  33.0 18.0 %all-to-all-done.1.got_ref = bf16[16,16,384]{2,1,0:T(8,128)(2,1)S(1)} async-done(((bf16[16,16,384]{2,1,0:T(8,128)(2,1)}), bf16[16,16,384]{2,1,0:T(8,128)(2,1)S(1)}, u32[]{:S(2)}, u32[]{:S(2)}) %all-to-all-start.1) | async-done | bytes 196640 | tf_op jit(solution)/shard_map/all_to_all | solution.py:230
  51.0 1.3 %shard_map.141 = bf16[32,16,128]{2,1,0:T(8,128)(2,1)S(1)} custom-call(bf16[16,16,384]{2,1,0:T(8,128)(2,1)S(1)} %all-to-all-done.1.got_ref, f32[64,512]{1,0:T(8,128)S(1)} %copy.34.bias_ref, f32[64,512]{1,0:T(8,128)S(1)} %copy.35.gate_ref, bf16[128,1024]{1,0:T(8,128)(2,1)S(1)} %fusion.10.select_ref), custom_call_target="tpu_custom_call" | custom-call | flops 1048576 | bytes 262144 | tf_op jit(solution)/shard_map/pallas_call | solution.py:241
  52.4 12.8 %all_to_all.20.heard_ref = bf16[32,16,128]{2,1,0:T(8,128)(2,1)S(1)} all-to-all(bf16[32,16,128]{2,1,0:T(8,128)(2,1)S(1)} %shard_map.141), channel_id=1, replica_groups=mesh['row'=16,'col'=32] {'col'}, dimensions={0} | all-to-all | bytes 262144 | tf_op jit(solution)/shard_map/all_to_all | solution.py:245
  65.2 1.0 shard_map.142
  66.2 8.1 %all-to-all-start.3 = ((bf16[32,16,128]{2,1,0:T(8,128)(2,1)}), bf16[32,16,128]{2,1,0:T(8,128)(2,1)S(1)}, u32[]{:S(2)}, u32[]{:S(2)}) async-start(bf16[32,16,128]{2,1,0:T(8,128)(2,1)} %shard_map.142), calls=%async_computation.3 | async-start | bytes 262144 | tf_op jit(solution)/shard_map/all_to_all | solution.py:247
  74.5 2.9 %collective-permute-start = (bf16[16,32,128]{2,1,0:T(8,128)(2,1)S(1)}, bf16[16,32,128]{2,1,0:T(8,128)(2,1)S(1)}, u32[]{:S(2)}, u32[]{:S(2)}) collective-permute-start(bf16[16,32,128]{2,1,0:T(8,128)(2,1)S(1)} %fusion.24), channel_id=1, source_target_pairs={{0,0},{1,1},{2,32},{3,33},{4,64},{5,65},{6,96},{7,97},{8,128},{9,1... | collective-permute-start | bytes 393224 | tf_op jit(solution)/shard_map/ppermute | solution.py:227
  77.5 13.2 %collective-permute-start.3 = (bf16[16,32,128]{2,1,0:T(8,128)(2,1)S(1)}, bf16[16,32,128]{2,1,0:T(8,128)(2,1)S(1)}, u32[]{:S(2)}, u32[]{:S(2)}) collective-permute-start(bf16[16,32,128]{2,1,0:T(8,128)(2,1)S(1)} %get-tuple-element.18), channel_id=1, source_target_pairs={{0,1},{1,0},{2,33},{3,32},{4,65},{5,64},{6,97},{7,96},{8,129},{9,1... | collective-permute-start | bytes 393224 | tf_op jit(solution)/shard_map/ppermute | solution.py:227
  90.7 3.2 %collective-permute-start.2 = (bf16[16,32,128]{2,1,0:T(8,128)(2,1)S(1)}, bf16[16,32,128]{2,1,0:T(8,128)(2,1)S(1)}, u32[]{:S(2)}, u32[]{:S(2)}) collective-permute-start(bf16[16,32,128]{2,1,0:T(8,128)(2,1)S(1)} %get-tuple-element.19), channel_id=1, source_target_pairs={{0,1},{1,0},{2,33},{3,32},{4,65},{5,64},{6,97},{7,96},{8,129},{9,1... | collective-permute-start | bytes 393224 | tf_op jit(solution)/shard_map/ppermute | solution.py:227
  93.9 13.7 %collective-permute-start.1 = (bf16[16,32,128]{2,1,0:T(8,128)(2,1)S(1)}, bf16[16,32,128]{2,1,0:T(8,128)(2,1)S(1)}, u32[]{:S(2)}, u32[]{:S(2)}) collective-permute-start(bf16[16,32,128]{2,1,0:T(8,128)(2,1)S(1)} %get-tuple-element.20), channel_id=1, source_target_pairs={{0,0},{1,1},{2,32},{3,33},{4,64},{5,65},{6,96},{7,97},{8,128},{9,1... | collective-permute-start | bytes 393224 | tf_op jit(solution)/shard_map/ppermute | solution.py:227
  108.2 7.4 %collective-permute-done.3.refs_3_ = bf16[16,32,128]{2,1,0:T(8,128)(2,1)S(1)} collective-permute-done((bf16[16,32,128]{2,1,0:T(8,128)(2,1)S(1)}, bf16[16,32,128]{2,1,0:T(8,128)(2,1)S(1)}, u32[]{:S(2)}, u32[]{:S(2)}) %collective-permute-start.3) | collective-permute-done | bytes 131104 | tf_op jit(solution)/shard_map/ppermute | solution.py:227
  115.6 5.3 %collective-permute-done.2.refs_2_ = bf16[16,32,128]{2,1,0:T(8,128)(2,1)S(1)} collective-permute-done((bf16[16,32,128]{2,1,0:T(8,128)(2,1)S(1)}, bf16[16,32,128]{2,1,0:T(8,128)(2,1)S(1)}, u32[]{:S(2)}, u32[]{:S(2)}) %collective-permute-start.2) | collective-permute-done | bytes 131104 | tf_op jit(solution)/shard_map/ppermute | solution.py:227
  121.0 3.3 %collective-permute-done.1.refs_1_ = bf16[16,32,128]{2,1,0:T(8,128)(2,1)S(1)} collective-permute-done((bf16[16,32,128]{2,1,0:T(8,128)(2,1)S(1)}, bf16[16,32,128]{2,1,0:T(8,128)(2,1)S(1)}, u32[]{:S(2)}, u32[]{:S(2)}) %collective-permute-start.1) | collective-permute-done | bytes 131104 | tf_op jit(solution)/shard_map/ppermute | solution.py:227
  124.3 0.7 copy-done.5
  125.0 3.5 %mlp.1 = bf16[64,32,128]{2,1,0:T(8,128)(2,1)} custom-call(s32[1]{0:T(128)} %bitcast.7.odd_ref, bf16[64,32,128]{2,1,0:T(8,128)(2,1)S(1)} %copy.36.zed_ref, bf16[64,32,128]{2,1,0:T(8,128)(2,1)S(1)} %copy-done.1, bf16[16,32,128]{2,1,0:T(8,128)(2,1)S(1)} %collective-permute-done.refs_0_, bf16[16,32,128]{2,1,0:T(8,128)(2,1)S(1)} %collective-permute-done.1.refs_1_, ...), custom_call_target="tpu_custom_call" | custom-call | flops 536870912 | bytes 2097152 | tf_op jit(solution)/shard_map/mlp/pallas_call | solution.py:266
  128.5 0.8 shard_map.143
  (43 shorter events, 3.2 us)
Async XLA Ops:
  0.6 30.3 %copy-start = (bf16[128,16]{0,1:T(8,128)(2,1)S(1)}, bf16[128,16]{0,1:T(8,128)(2,1)}, u32[]{:S(2)}) copy-start(bf16[128,16]{0,1:T(8,128)(2,1)} %param.19) | copy-start | bytes 12292
  0.6 10.2 %copy-start.1 = (bf16[64,32,128]{2,1,0:T(8,128)(2,1)S(1)}, bf16[64,32,128]{2,1,0:T(8,128)(2,1)}, u32[]{:S(2)}) copy-start(bf16[64,32,128]{2,1,0:T(8,128)(2,1)} %pair_ref.1) | copy-start | bytes 1572868
  2.6 12.7 %all-to-all-start = ((bf16[32,16,96]{2,1,0:T(8,128)(2,1)}), bf16[32,16,96]{2,1,0:T(8,128)(2,1)S(1)}, u32[]{:S(2)}, u32[]{:S(2)}) async-start(bf16[32,16,96]{2,1,0:T(8,128)(2,1)} %get-tuple-element.10), calls=%async_computation | async-start | bytes 262144 | tf_op jit(solution)/shard_map/all_to_all | solution.py:215
  12.5 0.7 copy-start.8
  13.2 2.2 %copy-start.4 = (bf16[2,16,96]{2,1,0:T(8,128)(2,1)S(1)}, bf16[2,16,96]{2,1,0:T(8,128)(2,1)}, u32[]{:S(2)}) copy-start(bf16[2,16,96]{2,1,0:T(8,128)(2,1)} %get-tuple-element.11.own_ref) | copy-start | bytes 18436
  16.2 34.9 %all-to-all-start.1 = ((bf16[16,16,384]{2,1,0:T(8,128)(2,1)}), bf16[16,16,384]{2,1,0:T(8,128)(2,1)S(1)}, u32[]{:S(2)}, u32[]{:S(2)}) async-start(bf16[16,16,384]{2,1,0:T(8,128)(2,1)} %shard_map.140), calls=%async_computation.1 | async-start | bytes 393216 | tf_op jit(solution)/shard_map/all_to_all | solution.py:230
  31.5 0.7 copy-start.9
  31.5 0.7 copy-start.10
  66.2 62.3 %all-to-all-start.3 = ((bf16[32,16,128]{2,1,0:T(8,128)(2,1)}), bf16[32,16,128]{2,1,0:T(8,128)(2,1)S(1)}, u32[]{:S(2)}, u32[]{:S(2)}) async-start(bf16[32,16,128]{2,1,0:T(8,128)(2,1)} %shard_map.142), calls=%async_computation.3 | async-start | bytes 262144 | tf_op jit(solution)/shard_map/all_to_all | solution.py:247
  74.5 33.7 %collective-permute-start = (bf16[16,32,128]{2,1,0:T(8,128)(2,1)S(1)}, bf16[16,32,128]{2,1,0:T(8,128)(2,1)S(1)}, u32[]{:S(2)}, u32[]{:S(2)}) collective-permute-start(bf16[16,32,128]{2,1,0:T(8,128)(2,1)S(1)} %fusion.24), channel_id=1, source_target_pairs={{0,0},{1,1},{2,32},{3,33},{4,64},{5,65},{6,96},{7,97},{8,128},{9,1... | collective-permute-start | bytes 393224 | tf_op jit(solution)/shard_map/ppermute | solution.py:227
  77.5 38.1 %collective-permute-start.3 = (bf16[16,32,128]{2,1,0:T(8,128)(2,1)S(1)}, bf16[16,32,128]{2,1,0:T(8,128)(2,1)S(1)}, u32[]{:S(2)}, u32[]{:S(2)}) collective-permute-start(bf16[16,32,128]{2,1,0:T(8,128)(2,1)S(1)} %get-tuple-element.18), channel_id=1, source_target_pairs={{0,1},{1,0},{2,33},{3,32},{4,65},{5,64},{6,97},{7,96},{8,129},{9,1... | collective-permute-start | bytes 393224 | tf_op jit(solution)/shard_map/ppermute | solution.py:227
  90.7 30.3 %collective-permute-start.2 = (bf16[16,32,128]{2,1,0:T(8,128)(2,1)S(1)}, bf16[16,32,128]{2,1,0:T(8,128)(2,1)S(1)}, u32[]{:S(2)}, u32[]{:S(2)}) collective-permute-start(bf16[16,32,128]{2,1,0:T(8,128)(2,1)S(1)} %get-tuple-element.19), channel_id=1, source_target_pairs={{0,1},{1,0},{2,33},{3,32},{4,65},{5,64},{6,97},{7,96},{8,129},{9,1... | collective-permute-start | bytes 393224 | tf_op jit(solution)/shard_map/ppermute | solution.py:227
  93.9 14.1 %copy-start.7 = (bf16[768,24]{0,1:T(8,128)(2,1)S(1)}, bf16[768,24]{0,1:T(8,128)(2,1)}, u32[]{:S(2)}) copy-start(bf16[768,24]{0,1:T(8,128)(2,1)} %param.16) | copy-start | bytes 110596
  93.9 30.4 %collective-permute-start.1 = (bf16[16,32,128]{2,1,0:T(8,128)(2,1)S(1)}, bf16[16,32,128]{2,1,0:T(8,128)(2,1)S(1)}, u32[]{:S(2)}, u32[]{:S(2)}) collective-permute-start(bf16[16,32,128]{2,1,0:T(8,128)(2,1)S(1)} %get-tuple-element.20), channel_id=1, source_target_pairs={{0,0},{1,1},{2,32},{3,33},{4,64},{5,65},{6,96},{7,97},{8,128},{9,1... | collective-permute-start | bytes 393224 | tf_op jit(solution)/shard_map/ppermute | solution.py:227
  107.7 16.7 %copy-start.3 = (bf16[512,128]{1,0:T(8,128)(2,1)S(1)}, bf16[512,128]{1,0:T(8,128)(2,1)}, u32[]{:S(2)}) copy-start(bf16[512,128]{1,0:T(8,128)(2,1)} %refs_6_.1) | copy-start | bytes 393220
  108.0 16.3 %copy-start.2 = (bf16[256,512]{1,0:T(8,128)(2,1)S(1)}, bf16[256,512]{1,0:T(8,128)(2,1)}, u32[]{:S(2)}) copy-start(bf16[256,512]{1,0:T(8,128)(2,1)} %refs_4_.1) | copy-start | bytes 786436
  124.3 0.7 copy-start.5
  124.3 0.7 copy-start.6
